TPU v7x, 32 devices: a whole 2x2x4 slice. The times are simulated.
32 devices in a mesh: section: 2 (over core), dp: 16 (over z, y, x).
Axes of the slice: x: 2, y: 2, z: 4, core: 2. Of those that a mesh axis runs over, the one named last changes fastest.
Arguments:
- images: bfloat16 [64, 196, 512], P('dp'), may hold values from -6 to 6
- cotangent: bfloat16 [64, 196, 512], P('dp'), may hold values from -6 to 6
- image_count: int32 [16], P('dp'), may hold values from 1 to 4, as said below
- norm1_gain: float32 [2, 512], P('section'), may hold values from 0.5 to 1.5
- norm1_bias: float32 [2, 512], P('section'), may hold values from -3 to 3
- qkv_weight: bfloat16 [2, 512, 1536], P('section'), may hold values from -0.25 to 0.25
- query_bias: float32 [2, 512], P('section'), may hold values from -3 to 3
- value_bias: float32 [2, 512], P('section'), may hold values from -3 to 3
- bias_table: float32 [2, 169, 16], P('section'), may hold values from -4 to 4
- out_weight: bfloat16 [2, 512, 512], P('section'), may hold values from -0.75 to 0.75
- out_bias: float32 [2, 512], P('section'), may hold values from -3 to 3
- norm2_gain: float32 [2, 512], P('section'), may hold values from 0.5 to 1.5
- norm2_bias: float32 [2, 512], P('section'), may hold values from -3 to 3
- up_weight: bfloat16 [2, 512, 2048], P('section'), may hold values from -0.25 to 0.25
- up_bias: float32 [2, 2048], P('section'), may hold values from -3 to 3
- down_weight: bfloat16 [2, 2048, 512], P('section'), may hold values from -0.125 to 0.125
- down_bias: float32 [2, 512], P('section'), may hold values from -3 to 3
Outputs:
- segment_out: bfloat16 [2, 64, 196, 512], P('section', 'dp')
- input_grad: float32 [2, 64, 196, 512], P('section', 'dp')
- grad_norm1_gain: float32 [2, 512], P('section')
- grad_norm1_bias: float32 [2, 512], P('section')
- grad_qkv_weight: float32 [2, 512, 1536], P('section')
- grad_query_bias: float32 [2, 512], P('section')
- grad_value_bias: float32 [2, 512], P('section')
- grad_bias_table: float32 [2, 169, 16], P('section')
- grad_out_weight: float32 [2, 512, 512], P('section')
- grad_out_bias: float32 [2, 512], P('section')
- grad_norm2_gain: float32 [2, 512], P('section')
- grad_norm2_bias: float32 [2, 512], P('section')
- grad_up_weight: float32 [2, 512, 2048], P('section')
- grad_up_bias: float32 [2, 2048], P('section')
- grad_down_weight: float32 [2, 2048, 512], P('section')
- grad_down_bias: float32 [2, 512], P('section')
Inputs may be any that keep to these rules, and one draw needn't show every extreme that they name: image_count of every dp index lies in 1 to 4; some index has all 4 slots live.
All inputs are finite; a program needn't handle non-finite values.
Results may differ from a plain program's by a relative error of at most 0.015.
Values may be sent and summed in bfloat16 or wider, within the bound.
No kernel may reach another device: no remote copies, remote signals or barrier semaphores. Data moves between devices by JAX's collectives and lax.ppermute only.
A program may use at most 192 MiB of HBM per device.

v0:
```python
import functools

import jax
import jax.numpy as jnp
import numpy as np
from jax import lax
from jax.experimental import pallas as pl
from jax.experimental.pallas import tpu as pltpu
from jax.sharding import PartitionSpec as P


WIN = 7
SIDE = 14
SHIFT = 3
CELLS = WIN * WIN
PADW = 64
NWIN = (SIDE // WIN) ** 2
IROWS = NWIN * PADW
GROUP = 4
LANES = 128
FCHUNK = 512
EPS = 1e-05
MASKED = -100.0
PADDED = -1e30
SQRT_HALF = 0.7071067811865476
INV_ROOT_TAU = 0.3989422804014327
F32 = jnp.float32
BF16 = jnp.bfloat16
SMALL_ROWS = 16
EXTRA = 32


def window_source(offset):
    across = SIDE // WIN
    places = np.arange(SIDE * SIDE)
    window_no = places // CELLS
    cell_no = places % CELLS
    grid_row = window_no // across * WIN + cell_no // WIN
    grid_col = window_no % across * WIN + cell_no % WIN
    source = (grid_row + offset) % SIDE * SIDE + (grid_col + offset) % SIDE
    return window_no * PADW + cell_no, source


def window_onehot(offset):
    rows, source = window_source(offset)
    table = np.zeros((IROWS, SIDE * SIDE), np.float32)
    table[rows, source] = 1.0
    return table


def region_mask():
    places = np.arange(SIDE)
    labels = (places >= SIDE - WIN).astype(np.int32) + (places >= SIDE - SHIFT).astype(np.int32)
    region = (labels[:, None] * 3 + labels[None, :]).reshape(-1)
    rows, source = window_source(0)
    padded = np.full((IROWS,), -1)
    padded[rows] = region[source]
    padded = padded.reshape(NWIN, PADW)
    differ = (padded[:, :, None] != padded[:, None, :]) & (padded[:, :, None] >= 0)
    differ &= padded[:, None, :] >= 0
    return np.where(differ, MASKED, 0.0).astype(np.float32)


def relative_index():
    cells = np.arange(CELLS)
    row_of, col_of = cells // WIN, cells % WIN
    row_gap = row_of[:, None] - row_of[None, :] + WIN - 1
    return row_gap * (2 * WIN - 1) + col_of[:, None] - col_of[None, :] + WIN - 1


def pair_onehot():
    index = np.full((PADW, PADW), -1, np.int32)
    index[:CELLS, :CELLS] = relative_index().T
    entries = lax.broadcasted_iota(jnp.int32, ((2 * WIN - 1) ** 2, PADW * PADW), 0)
    return (entries == jnp.asarray(index.reshape(1, -1))).astype(BF16)


def three_terms(value):
    high = lax.reduce_precision(value, 8, 7)
    mid = lax.reduce_precision(value - high, 8, 7)
    return jnp.stack([high, mid, value - high - mid]).astype(BF16)


def bias_tiles(tables, onehot):
    layers, _, heads = tables.shape
    terms = three_terms(tables.transpose(0, 2, 1)).reshape(3 * layers * heads, -1)
    spread = dot_nn(terms, onehot).reshape(3, layers * heads, -1).sum(axis=0)
    tiles = spread.reshape(layers, heads // GROUP, GROUP, PADW, PADW).transpose(0, 1, 3, 2, 4)
    pad_key = np.where(np.arange(PADW) >= CELLS, PADDED, 0.0).astype(np.float32)
    tiles = tiles + pad_key[None, None, :, None, None]
    plain = tiles[0][None]
    masked = tiles[1][None] + region_mask()[:, None, :, None, :]
    return [part.reshape(part.shape[0], heads // GROUP, PADW, GROUP * PADW) for part in (plain, masked)]


def table_grad(tiles, heads, onehot):
    spread = tiles.reshape(heads // GROUP, PADW, GROUP, PADW).transpose(0, 2, 1, 3)
    terms = three_terms(spread.reshape(heads, PADW * PADW)).reshape(3 * heads, -1)
    return dot_nt(terms, onehot).reshape(3, heads, -1).sum(axis=0)


def dot_nn(left, right):
    return lax.dot_general(left, right, (((1,), (0,)), ((), ())), preferred_element_type=F32)


def dot_nt(left, right):
    return lax.dot_general(left, right, (((1,), (1,)), ((), ())), preferred_element_type=F32)


def dot_tn(left, right):
    return lax.dot_general(left, right, (((0,), (0,)), ((), ())), preferred_element_type=F32)


def normalize(values):
    centered = values - jnp.mean(values, axis=-1, keepdims=True)
    inv_std = lax.rsqrt(jnp.mean(centered * centered, axis=-1, keepdims=True) + EPS)
    return centered * inv_std, inv_std


def norm_back(upstream, scaled, inv_std, gain):
    along = upstream * gain
    return inv_std * (
        along
        - jnp.mean(along, axis=-1, keepdims=True)
        - scaled * jnp.mean(along * scaled, axis=-1, keepdims=True)
    )


def gelu_parts(pre):
    cdf_val = 0.5 * (1.0 + lax.erf(pre * SQRT_HALF))
    density = jnp.exp(-0.5 * pre * pre) * INV_ROOT_TAU
    return pre * cdf_val, cdf_val + pre * density


def head_mask(head_dim):
    rows = lax.broadcasted_iota(jnp.int32, (GROUP * PADW, LANES), 0) // PADW
    cols = lax.broadcasted_iota(jnp.int32, (GROUP * PADW, LANES), 1) // head_dim
    return jnp.where(rows == cols, 1.0, 0.0).astype(BF16)


def expand(tile, mask):
    return jnp.concatenate([tile] * GROUP, axis=0) * mask


def collapse(wide, head_dim):
    head_of = lax.broadcasted_iota(jnp.int32, (PADW, LANES), 1) // head_dim
    total = wide[:PADW]
    for head in range(1, GROUP):
        total = jnp.where(head_of == head, wide[head * PADW : (head + 1) * PADW], total)
    return total


def rows_at(number, size):
    return pl.ds(pl.multiple_of(number * size, size), size)


def forward_kernel(
    base_ref, x_ref, perm_ref, bias_ref, vec_ref, wqkv_ref, wout_ref, wup_ref, wdown_ref,
    out_ref, *refs, images, head_dim, masked, spill,
):
    kept = refs[9:18] if spill else refs
    xa_ref, nrm_ref, qkv_ref, prob_ref, mix_ref, res_ref, n2_ref, act_ref, slope_ref = kept

    def whole_copy(number):
        return pltpu.make_async_copy(kept[number], refs[number], refs[18].at[number])

    def image_copy(number, img):
        rows = rows_at(img, IROWS)
        return pltpu.make_async_copy(kept[number].at[rows, :], refs[number].at[rows, :], refs[19].at[number, img])

    width = wout_ref.shape[0]
    hidden = wup_ref.shape[1]
    groups = width // LANES
    factor = head_dim ** (-0.5)
    first = base_ref[0]

    def enter(img, carry):
        rows = rows_at(img, IROWS)
        entry = dot_nn(perm_ref[...], x_ref[first + img])
        xa_ref[rows, :] = entry.astype(BF16)
        scaled, _ = normalize(entry)
        normed = (scaled * vec_ref[0:1, :] + vec_ref[1:2, :]).astype(BF16)
        nrm_ref[rows, :] = normed
        query = (dot_nn(normed, wqkv_ref[:, :width]) + vec_ref[2:3, :]) * factor
        qkv_ref[rows, :width] = query.astype(BF16)
        qkv_ref[rows, width : 2 * width] = dot_nn(normed, wqkv_ref[:, width : 2 * width]).astype(BF16)
        value = dot_nn(normed, wqkv_ref[:, 2 * width :]) + vec_ref[3:4, :]
        qkv_ref[rows, 2 * width :] = value.astype(BF16)
        return carry

    lax.fori_loop(0, images, enter, 0)
    if spill:
        for number in range(3):
            whole_copy(number).start()
    mask = head_mask(head_dim)

    def attend(win, carry):
        rows = rows_at(win, PADW)
        bias_no = win % NWIN if masked else 0
        for grp in range(groups):
            at = grp * LANES
            query = qkv_ref[rows, at : at + LANES]
            key = qkv_ref[rows, width + at : width + at + LANES]
            value = qkv_ref[rows, 2 * width + at : 2 * width + at + LANES]
            score = dot_nt(key, expand(query, mask)) + bias_ref[bias_no, grp]
            expo = jnp.exp(score - jnp.max(score, axis=0, keepdims=True))
            prob = expo * (1.0 / jnp.sum(expo, axis=0, keepdims=True))
            prob_ref[win, grp] = prob
            wide = dot_tn(prob.astype(BF16), value)
            mix_ref[rows, at : at + LANES] = collapse(wide, head_dim).astype(BF16)
        return carry

    lax.fori_loop(0, images * NWIN, attend, 0)
    if spill:
        for number in range(3, 5):
            whole_copy(number).start()

    def leave(img, carry):
        rows = rows_at(img, IROWS)
        entry = xa_ref[rows, :].astype(F32)
        resid = entry + dot_nn(mix_ref[rows, :], wout_ref[...]) + vec_ref[4:5, :]
        res_ref[rows, :] = resid
        scaled, _ = normalize(resid)
        n2_ref[rows, :] = (scaled * vec_ref[5:6, :] + vec_ref[6:7, :]).astype(BF16)
        for part in range(hidden // FCHUNK):
            at = part * FCHUNK
            pre = dot_nn(n2_ref[rows, :], wup_ref[:, at : at + FCHUNK]) + vec_ref[8 + part : 9 + part, :]
            activ, slope = gelu_parts(pre)
            act_ref[rows, at : at + FCHUNK] = activ.astype(BF16)
            slope_ref[rows, at : at + FCHUNK] = slope.astype(BF16)
        done = res_ref[rows, :] + dot_nn(act_ref[rows, :], wdown_ref[...]) + vec_ref[7:8, :]
        out_ref[img] = dot_tn(perm_ref[...], done.astype(BF16)).astype(BF16)
        if spill:
            for number in range(5, 9):
                image_copy(number, img).start()
        return carry

    lax.fori_loop(0, images, leave, 0)
    if spill:
        for number in range(5):
            whole_copy(number).wait()
        for img in range(images):
            for number in range(5, 9):
                image_copy(number, img).wait()


def ffn_back_kernel(
    base_ref, g_ref, live_ref, perm_ref, vec_ref, wout_ref, wup_ref, wdown_ref,
    mix_ref, res_ref, n2_ref, act_ref, slope_ref,
    dres_ref, dmix_ref, keep_ref, send_ref,
    small_ref, gb_ref, dpre_ref, dresb_ref,
    *, images,
):
    width = wout_ref.shape[0]
    hidden = wup_ref.shape[1]
    first = base_ref[0]
    section = base_ref[1]
    small_ref[...] = jnp.zeros_like(small_ref)

    def step(img, carry):
        rows = rows_at(img, IROWS)
        upstream = dot_nn(perm_ref[...], g_ref[first + img]) * live_ref[img]
        gb_ref[rows, :] = upstream.astype(BF16)
        small_ref[7:8, :] += jnp.sum(upstream, axis=0, keepdims=True)
        for part in range(hidden // FCHUNK):
            at = part * FCHUNK
            slope = slope_ref[rows, at : at + FCHUNK].astype(F32)
            dpre = dot_nt(gb_ref[rows, :], wdown_ref[at : at + FCHUNK, :]) * slope
            small_ref[8 + part : 9 + part, :] += jnp.sum(dpre, axis=0, keepdims=True)
            dpre_ref[rows, at : at + FCHUNK] = dpre.astype(BF16)
        dnorm = dot_nt(dpre_ref[rows, :], wup_ref[...])
        scaled, inv_std = normalize(res_ref[rows, :])
        small_ref[5:6, :] += jnp.sum(dnorm * scaled, axis=0, keepdims=True)
        small_ref[6:7, :] += jnp.sum(dnorm, axis=0, keepdims=True)
        dres = gb_ref[rows, :].astype(F32) + norm_back(dnorm, scaled, inv_std, vec_ref[5:6, :])
        dres_ref[rows, :] = dres
        small_ref[4:5, :] += jnp.sum(dres, axis=0, keepdims=True)
        dresb_ref[rows, :] = dres.astype(BF16)
        dmix_ref[rows, :] = dot_nt(dresb_ref[rows, :], wout_ref[...]).astype(BF16)
        return carry

    lax.fori_loop(0, images, step, 0)
    span = hidden // 2
    for side, dest in ((0, keep_ref), (1, send_ref)):
        half = section if side == 0 else 1 - section

        def down(part, carry, half=half, dest=dest):
            cols = pl.ds(pl.multiple_of(half * span + part * FCHUNK, FCHUNK), FCHUNK)
            dest[rows_at(part, FCHUNK), :] = dot_tn(act_ref[:, cols], gb_ref[...]).astype(BF16)
            return carry

        lax.fori_loop(0, span // FCHUNK, down, 0, unroll=True)
        cols = rows_at(half, width // 2)

        def up(part, carry, cols=cols, dest=dest):
            block = dot_tn(n2_ref[:, cols], dpre_ref[:, rows_at(part, width)])
            place = pl.ds(pl.multiple_of(span + part * (width // 2), width // 2), width // 2)
            dest[place, :] = block.astype(BF16)
            return carry

        lax.fori_loop(0, hidden // width, up, 0, unroll=True)
        dest[2 * span :, :] = dot_tn(mix_ref[:, cols], dresb_ref[...]).astype(BF16)


def attn_back_kernel(
    base_ref, perm_ref, vec_ref, wqkv_ref, xa_ref, nrm_ref, qkv_ref, prob_ref, dres_ref, dmix_ref,
    igrad_ref, igrad_b_ref, keep_ref, send_ref, tiles_ref, small_ref, dqkv_ref,
    *, images, head_dim,
):
    width = wqkv_ref.shape[0]
    groups = width // LANES
    factor = head_dim ** (-0.5)
    section = base_ref[1]
    small_ref[...] = jnp.zeros_like(small_ref)
    tiles_ref[...] = jnp.zeros_like(tiles_ref)
    mask = head_mask(head_dim)

    def attend(win, carry):
        rows = rows_at(win, PADW)
        for grp in range(groups):
            at = grp * LANES
            query = qkv_ref[rows, at : at + LANES]
            key = qkv_ref[rows, width + at : width + at + LANES]
            value = qkv_ref[rows, 2 * width + at : 2 * width + at + LANES]
            dmix = expand(dmix_ref[rows, at : at + LANES], mask)
            prob = prob_ref[win, grp]
            dprob = dot_nt(value, dmix)
            dvalue = dot_nn(prob.astype(BF16), dmix)
            dscore = prob * (dprob - jnp.sum(prob * dprob, axis=0, keepdims=True))
            tiles_ref[grp] += dscore
            dscore_b = dscore.astype(BF16)
            dkey = dot_nn(dscore_b, expand(query, mask))
            dquery = collapse(dot_tn(dscore_b, key), head_dim) * factor
            small_ref[2:3, at : at + LANES] += jnp.sum(dquery, axis=0, keepdims=True)
            small_ref[3:4, at : at + LANES] += jnp.sum(dvalue, axis=0, keepdims=True)
            dqkv_ref[rows, at : at + LANES] = dquery.astype(BF16)
            dqkv_ref[rows, width + at : width + at + LANES] = dkey.astype(BF16)
            dqkv_ref[rows, 2 * width + at : 2 * width + at + LANES] = dvalue.astype(BF16)
        return carry

    lax.fori_loop(0, images * NWIN, attend, 0)

    def leave(img, carry):
        rows = rows_at(img, IROWS)
        dnorm = dot_nt(dqkv_ref[rows, :], wqkv_ref[...])
        scaled, inv_std = normalize(xa_ref[rows, :].astype(F32))
        small_ref[0:1, :] += jnp.sum(dnorm * scaled, axis=0, keepdims=True)
        small_ref[1:2, :] += jnp.sum(dnorm, axis=0, keepdims=True)
        grad = dres_ref[rows, :] + norm_back(dnorm, scaled, inv_std, vec_ref[0:1, :])
        high = grad.astype(BF16)
        low = (grad - high.astype(F32)).astype(BF16)
        moved = dot_tn(perm_ref[...], high)
        igrad_b_ref[img] = moved.astype(BF16)
        igrad_ref[img] = moved + dot_tn(perm_ref[...], low)
        return carry

    lax.fori_loop(0, images, leave, 0)
    for side, dest in ((0, keep_ref), (1, send_ref)):
        half = section if side == 0 else 1 - section
        cols = rows_at(half, width // 2)

        def part_grad(part, carry, cols=cols, dest=dest):
            block = dot_tn(nrm_ref[:, cols], dqkv_ref[:, rows_at(part, width)])
            dest[rows_at(part, width // 2), :] = block.astype(BF16)
            return carry

        lax.fori_loop(0, 3, part_grad, 0, unroll=True)


def vmem():
    return pl.BlockSpec(memory_space=pltpu.VMEM)


def smem():
    return pl.BlockSpec(memory_space=pltpu.SMEM)


def shape_of(shape, dtype):
    return jax.ShapeDtypeStruct(shape, dtype)


PARAMS = pltpu.CompilerParams(vmem_limit_bytes=16 * 1024 * 1024)
SPILL_PARAMS = pltpu.CompilerParams(vmem_limit_bytes=30 * 1024 * 1024)
SMALL_PARAMS = pltpu.CompilerParams(vmem_limit_bytes=16 * 1024 * 1024)


def busy(micros):
    return pl.CostEstimate(flops=micros * 1000000000, transcendentals=0, bytes_accessed=1000000)


def run_forward(base, rows_in, perm, bias, vec, weights, images, head_dim, masked):
    wqkv, wout, wup, wdown = weights
    width, hidden = wup.shape
    total = images * IROWS
    shapes = (
        shape_of((images, SIDE * SIDE, width), BF16),
        shape_of((total, width), BF16),
        shape_of((total, width), BF16),
        shape_of((total, 3 * width), BF16),
        shape_of((images * NWIN, width // LANES, PADW, GROUP * PADW), F32),
        shape_of((total, width), BF16),
        shape_of((total, width), F32),
        shape_of((total, width), BF16),
        shape_of((total, hidden), BF16),
        shape_of((total, hidden), BF16),
    )
    spill = not masked
    scratch = []
    if spill:
        scratch = [pltpu.VMEM(shape.shape, shape.dtype) for shape in shapes[1:]]
        scratch += [pltpu.SemaphoreType.DMA((5,)), pltpu.SemaphoreType.DMA((9, images))]
    return pl.pallas_call(
        functools.partial(forward_kernel, images=images, head_dim=head_dim, masked=masked, spill=spill),
        out_shape=shapes,
        in_specs=[smem()] + [vmem()] * 8,
        out_specs=(vmem(), *(pl.BlockSpec(memory_space=pl.ANY) if spill else vmem() for _ in shapes[1:])),
        scratch_shapes=scratch,
        compiler_params=SPILL_PARAMS if spill else PARAMS,
        cost_estimate=busy(13),
        name="layer_forward",
    )(base, rows_in, perm, bias, vec, wqkv, wout, wup, wdown)


def run_ffn_back(base, g_rows, live, perm, vec, weights, kept, images):
    _, wout, wup, wdown = weights
    _, _, _, _, mix, res, n2, act, slope = kept
    width, hidden = wup.shape
    total = images * IROWS
    shapes = (
        shape_of((total, width), F32),
        shape_of((total, width), BF16),
        shape_of((hidden + width // 2, width), BF16),
        shape_of((hidden + width // 2, width), BF16),
        shape_of((SMALL_ROWS, width), F32),
    )
    return pl.pallas_call(
        functools.partial(ffn_back_kernel, images=images),
        out_shape=shapes,
        in_specs=[smem(), vmem(), smem()] + [vmem()] * 10,
        out_specs=tuple(vmem() for _ in shapes),
        scratch_shapes=[
            pltpu.VMEM((total, width), BF16),
            pltpu.VMEM((total, hidden), BF16),
            pltpu.VMEM((total, width), BF16),
        ],
        compiler_params=PARAMS,
        cost_estimate=busy(9),
        name="ffn_back",
    )(base, g_rows, live, perm, vec, wout, wup, wdown, mix, res, n2, act, slope)


def run_attn_back(base, perm, vec, weights, kept, dres, dmix, images, head_dim):
    wqkv = weights[0]
    xa, nrm, qkv, prob = kept[:4]
    width = wqkv.shape[0]
    total = images * IROWS
    shapes = (
        shape_of((images, SIDE * SIDE, width), F32),
        shape_of((images, SIDE * SIDE, width), BF16),
        shape_of((3 * width // 2, width), BF16),
        shape_of((3 * width // 2, width), BF16),
        shape_of((width // LANES, PADW, GROUP * PADW), F32),
        shape_of((SMALL_ROWS, width), F32),
    )
    return pl.pallas_call(
        functools.partial(attn_back_kernel, images=images, head_dim=head_dim),
        out_shape=shapes,
        in_specs=[smem()] + [vmem()] * 9,
        out_specs=tuple(vmem() for _ in shapes),
        scratch_shapes=[pltpu.VMEM((total, 3 * width), BF16)],
        compiler_params=PARAMS,
        cost_estimate=busy(13),
        name="attn_back",
    )(base, perm, vec, wqkv, xa, nrm, qkv, prob, dres, dmix)


def round_orders(bits):
    if bits == 4:
        return ((0, 1, 2, 3), (1, 0, 3, 2), (2, 3, 0, 1), (3, 2, 0, 1))
    axes = list(range(bits))
    return tuple(tuple(axes[turn:] + axes[:turn]) for turn in range(4))


def added(left, right):
    return (left.astype(F32) + right.astype(F32)).astype(BF16)


def first_ffn_kernel(bit_ref, keep_ref, recv_ref, *outs, turn):
    tail_ref = outs[4]
    for color in range(2):
        half = outs[color].shape[0]
        bit = bit_ref[turn + color]
        for side, place in ((0, bit), (2, 1 - bit)):
            rows = pl.ds(pl.multiple_of(color * 2 * half + place * half, half), half)
            outs[side + color][...] = added(keep_ref[rows, :], recv_ref[rows, :])
    tail = keep_ref.shape[0] - tail_ref.shape[0]
    tail_ref[...] = added(keep_ref[tail:, :], recv_ref[tail:, :])


def first_qkv_kernel(bit_ref, tail_ref, keep_ref, recv_ref, *outs, turn):
    half = outs[0].shape[0]
    head = added(keep_ref[:half, :], recv_ref[:half, :])
    low = bit_ref[turn + 2] == 0
    outs[0][...] = jnp.where(low, tail_ref[...], head)
    outs[2][...] = jnp.where(low, head, tail_ref[...])
    bit = bit_ref[turn + 3]
    for side, place in ((1, bit), (3, 1 - bit)):
        rows = pl.ds(pl.multiple_of(half + place * half, half), half)
        outs[side][...] = added(keep_ref[rows, :], recv_ref[rows, :])


def sum_kernel(bit_ref, *refs, turn):
    keep, recv, outs = refs[:4], refs[4:8], refs[8:]
    for color in range(4):
        half = keep[color].shape[0] // 2
        bit = bit_ref[turn + color]
        for side, start in ((0, bit * half), (4, (1 - bit) * half)):
            rows = pl.ds(pl.multiple_of(start, 8), half)
            outs[side + color][...] = added(keep[color][rows, :], recv[color][rows, :])


def last_kernel(bit_ref, *refs, turn):
    keep, recv, out_ref = refs[:4], refs[4:8], refs[8]
    at = 0
    for color in range(4):
        size = keep[color].shape[0]
        out_ref[at : at + size, :] = added(keep[color][...], recv[color][...])
        at += size


def split_small(value):
    high = value.astype(BF16)
    return high, (value - high.astype(F32)).astype(BF16)


def pick_kernel(section_ref, zero_ref, one_ref, small_zero_ref, small_one_ref, own_ref, send_ref, *, turn):
    first = section_ref[0] == 0
    size = zero_ref.shape[0]
    own_ref[:size, :] = jnp.where(first, zero_ref[...], one_ref[...])
    send_ref[:size, :] = jnp.where(first, one_ref[...], zero_ref[...])
    for dest, value in (
        (own_ref, jnp.where(first, small_zero_ref[...], small_one_ref[...])),
        (send_ref, jnp.where(first, small_one_ref[...], small_zero_ref[...])),
    ):
        high, low = split_small(value)
        dest[size : size + EXTRA, :] = high
        dest[size + EXTRA :, :] = low


def join_kernel(section_ref, own_ref, got_ref, *outs, turn):
    first = section_ref[0] == 0
    at = 0
    for color in range(4):
        size = outs[color].shape[1] - (EXTRA if color == 3 else 0)
        mine, other = own_ref[at : at + size, :], got_ref[at : at + size, :]
        outs[color][0, :size, :] = jnp.where(first, mine, other)
        outs[color][1, :size, :] = jnp.where(first, other, mine)
        at += size
    total = jnp.zeros((EXTRA, own_ref.shape[1]), F32)
    for ref in (own_ref, got_ref):
        total += ref[at : at + EXTRA, :].astype(F32) + ref[at + EXTRA :, :].astype(F32)
    high, low = split_small(total)
    outs[3][0, size:, :] = high
    outs[3][1, size:, :] = low


def small_total(own_ref, recv_ref):
    total = jnp.zeros((EXTRA, own_ref.shape[2]), F32)
    at = own_ref.shape[1] - EXTRA
    for ref in (own_ref, recv_ref):
        total += ref[0, at:, :].astype(F32) + ref[1, at:, :].astype(F32)
    return total


def merge_kernel(bit_ref, *refs, turn):
    own, recv, outs = refs[:4], refs[4:8], refs[8:]
    for color in range(4):
        size = own[color].shape[1] - (EXTRA if color == 3 else 0)
        bit = bit_ref[turn + color]
        outs[color][:, pl.ds(pl.multiple_of(bit * size, 8), size), :] = own[color][:, :size, :]
        outs[color][:, pl.ds(pl.multiple_of((1 - bit) * size, 8), size), :] = recv[color][:, :size, :]
    high, low = split_small(small_total(own[3], recv[3]))
    outs[3][0, 2 * size :, :] = high
    outs[3][1, 2 * size :, :] = low


def final_kernel(bit_ref, *refs, turn):
    own, recv = refs[:4], refs[4:8]
    down_ref, up_ref, out_ref, qkv_ref = refs[8:12]
    rows_refs, up_bias_ref, table_ref = refs[12:20], refs[20], refs[21]
    width = out_ref.shape[1]
    part = width // 2
    for half in range(2):
        rows = slice(half * part, (half + 1) * part)
        bit = bit_ref[turn + 0]
        span = own[0].shape[1]
        for side, source in ((bit, own[0]), (1 - bit, recv[0])):
            down_ref[pl.ds(pl.multiple_of(half * 2 * span + side * span, span), span), :] = source[half].astype(F32)
        bit = bit_ref[turn + 1]
        blocks = own[1].shape[1] // part
        for side, source in ((bit, own[1]), (1 - bit, recv[1])):
            for block in range(blocks):
                cols = pl.ds(pl.multiple_of((side * blocks + block) * width, width), width)
                up_ref[rows, cols] = source[half, block * part : (block + 1) * part, :].astype(F32)
        is_low = bit_ref[turn + 2] == 0
        mine, other = own[2][half].astype(F32), recv[2][half].astype(F32)
        out_ref[rows, :] = jnp.where(is_low, mine, other)
        qkv_ref[rows, :width] = jnp.where(is_low, other, mine)
        bit = bit_ref[turn + 3]
        size = own[3].shape[1] - EXTRA
        for side, source in ((bit, own[3]), (1 - bit, recv[3])):
            cols = pl.ds(pl.multiple_of((1 + side) * width, width), width)
            qkv_ref[rows, cols] = source[half, :size, :].astype(F32)
    total = small_total(own[3], recv[3])
    for number, ref in enumerate(rows_refs):
        ref[...] = total[number : number + 1, :]
    for block in range(up_bias_ref.shape[1] // width):
        up_bias_ref[:, block * width : (block + 1) * width] = total[8 + block : 9 + block, :]
    table_ref[...] = total[SMALL_ROWS:, : table_ref.shape[1]]


def small_call(kernel, bits, arrays, shapes, turn=0):
    return pl.pallas_call(
        functools.partial(kernel, turn=4 * turn),
        out_shape=tuple(shapes),
        in_specs=[smem()] + [vmem()] * len(arrays),
        out_specs=tuple(vmem() for _ in shapes),
        compiler_params=SMALL_PARAMS,
    )(bits, *arrays)


def exchange(value, bit, count):
    return lax.ppermute(value, "dp", [(one, one ^ (1 << bit)) for one in range(count)])


def start_rounds(keep_ffn, send_ffn, keep_qkv, send_qkv, place_bits):
    width = keep_ffn.shape[1]
    recv_ffn = swap(send_ffn)
    recv_qkv = swap(send_qkv)
    long = shape_of(((keep_ffn.shape[0] - width // 2) // 4, width), BF16)
    short = shape_of((width // 2, width), BF16)
    *ffn, tail = small_call(first_ffn_kernel, place_bits, (keep_ffn, recv_ffn), [long] * 4 + [short])
    rest = small_call(first_qkv_kernel, place_bits, (tail, keep_qkv, recv_qkv), [short] * 4)
    return (*ffn[:2], *rest[:2], *ffn[2:], *rest[2:])


def reduce_rounds(parts, orders, place_bits, count):
    width = parts[0].shape[1]
    rounds = len(orders[0])
    for turn in range(rounds):
        mine, gone = parts[:4], parts[4:]
        recv = [exchange(part, order[turn], count) for part, order in zip(gone, orders)]
        if turn + 1 < rounds:
            halves = [shape_of((part.shape[0] // 2, width), BF16) for part in mine]
            parts = small_call(sum_kernel, place_bits, list(mine) + recv, halves * 2, turn + 1)
        else:
            total = shape_of((sum(part.shape[0] for part in mine), width), BF16)
            parts = small_call(last_kernel, place_bits, list(mine) + recv, [total])
    return parts[0]


def gather_layer(shard_zero, shard_one, small_zero, small_one, where, sizes, hidden, entries, heads, orders, place_bits, count):
    rows, width = shard_zero.shape
    both_shape = [shape_of((rows + 2 * EXTRA, width), BF16)] * 2
    own, send = small_call(pick_kernel, where, (shard_zero, shard_one, small_zero, small_one), both_shape)
    got = swap(send)
    extras = (0, 0, 0, EXTRA)
    shapes = [shape_of((2, size + extra, width), BF16) for size, extra in zip(sizes, extras)]
    parts = small_call(join_kernel, where, (own, got), shapes)
    rounds = len(orders[0])
    for turn in reversed(range(rounds)):
        recv = [exchange(part, order[turn], count) for part, order in zip(parts, orders)]
        if turn:
            shapes = [
                shape_of((2, 2 * part.shape[1] - extra, width), BF16) for part, extra in zip(parts, extras)
            ]
            parts = small_call(merge_kernel, place_bits, list(parts) + recv, shapes, turn)
    shapes = [shape_of((hidden, width), F32), shape_of((width, hidden), F32), shape_of((width, width), F32),
              shape_of((width, 3 * width), F32)]
    shapes += [shape_of((1, width), F32)] * 8 + [shape_of((1, hidden), F32), shape_of((heads, entries), F32)]
    return small_call(final_kernel, place_bits, list(parts) + recv, shapes)


def swap(value):
    return lax.ppermute(value, "section", [(0, 1), (1, 0)])


def both(value, section):
    other = swap(value)
    first = jnp.where(section == 0, value, other)
    second = jnp.where(section == 0, other, value)
    return first, second


def body(
    images,
    cotangent,
    image_count,
    norm1_gain,
    norm1_bias,
    qkv_weight,
    query_bias,
    value_bias,
    bias_table,
    out_weight,
    out_bias,
    norm2_gain,
    norm2_bias,
    up_weight,
    up_bias,
    down_weight,
    down_bias,
):
    section = lax.axis_index("section")
    slots = images.shape[0]
    mine = slots // 2
    width = images.shape[-1]
    heads = bias_table.shape[-1]
    head_dim = width // heads
    vectors = jnp.concatenate(
        [norm1_gain, norm1_bias, query_bias, value_bias, out_bias, norm2_gain, norm2_bias, down_bias,
         up_bias.reshape(-1, width)], axis=0)
    layer_vec = both(vectors, section)
    layer_table = both(bias_table[0], section)
    layer_w = list(zip(*[both(weight[0], section) for weight in (qkv_weight, out_weight, up_weight, down_weight)]))
    perms = [jnp.asarray(window_onehot(shift), BF16) for shift in (0, SHIFT)]
    onehot = pair_onehot()
    biases = bias_tiles(jnp.stack(layer_table), onehot)
    base_mine = jnp.stack([section * mine, section]).astype(jnp.int32)
    base_zero = jnp.stack([section * 0, section]).astype(jnp.int32)
    live = (section * mine + jnp.arange(mine) < image_count[0]).astype(F32)
    ones = jnp.ones((mine,), F32)
    count = lax.axis_size("dp")
    bits = count.bit_length() - 1
    chip = lax.axis_index("dp")
    orders = round_orders(bits)
    turns = np.array([[order[turn] for order in orders] for turn in range(bits)]).reshape(-1)
    place_bits = (chip >> turns.astype(np.int32)) & 1

    out_zero, *kept_zero = run_forward(base_mine, images, perms[0], biases[0], layer_vec[0], layer_w[0], mine, head_dim, False)
    out_one, *kept_one = run_forward(base_zero, out_zero, perms[1], biases[1], layer_vec[1], layer_w[1], mine, head_dim, True)

    def backward(layer, base, g_rows, alive, kept):
        dres, dmix, keep_ffn, send_ffn, small_ffn = run_ffn_back(
            base, g_rows, alive, perms[layer], layer_vec[layer], layer_w[layer], kept, mine)
        igrad, igrad_b, keep_qkv, send_qkv, tiles, small_attn = run_attn_back(
            base, perms[layer], layer_vec[layer], layer_w[layer], kept, dres, dmix, mine, head_dim)
        parts = start_rounds(keep_ffn, send_ffn, keep_qkv, send_qkv, place_bits)
        shard = reduce_rounds(parts, orders, place_bits, count)
        return igrad, igrad_b, shard, (tiles, small_ffn + small_attn), parts

    igrad_one, back_rows, shard_one, rest_one, parts = backward(1, base_mine, cotangent, live, kept_one)
    halves = [part.shape[0] for part in parts[:4]]
    igrad_zero, _, shard_zero, rest_zero, parts = backward(0, base_zero, back_rows, ones, kept_zero)

    def finish_small(rest):
        (tiles, vecs), _ = lax.optimization_barrier((rest, parts[2]))
        table = table_grad(tiles, heads, onehot)
        return jnp.concatenate([vecs, jnp.pad(table, ((0, 0), (0, width - table.shape[1])))])

    small_zero, small_one = finish_small(rest_zero), finish_small(rest_one)

    hidden = up_bias.shape[1]
    sizes = [half >> (bits - 1) for half in halves]
    where = section.astype(jnp.int32).reshape(1)
    g_down, g_up, g_out, g_qkv, *vecs, g_up_b, g_table = gather_layer(
        shard_zero, shard_one, small_zero, small_one, where, sizes, hidden, bias_table.shape[1], heads, orders,
        place_bits, count)

    def place(first, second):
        got = swap(jnp.where(section == 0, second, first))
        upper = jnp.concatenate([first, got], axis=0)
        lower = jnp.concatenate([got, second], axis=0)
        return jnp.where(section == 0, upper, lower)

    segment_out = place(out_zero, out_one)
    input_grad = place(igrad_zero, igrad_one)
    g_gain_one, g_bias_one, g_query, g_value, g_out_b, g_gain_two, g_bias_two, g_down_b = vecs
    return (
        segment_out[None], input_grad[None], g_gain_one, g_bias_one, g_qkv[None], g_query, g_value, g_table.T[None],
        g_out[None], g_out_b, g_gain_two, g_bias_two, g_up[None], g_up_b, g_down[None], g_down_b,
    )


def solution(mesh):
    row = P("section", None)
    mat = P("section", None, None)

    return jax.shard_map(
        body,
        mesh=mesh,
        in_specs=(
            P("dp", None, None), P("dp", None, None), P("dp"),
            row, row, mat, row, row, mat, mat, row, row, row, mat, row, mat, row,
        ),
        out_specs=(
            P("section", "dp", None, None), P("section", "dp", None, None),
            row, row, mat, row, row, mat, mat, row, row, row, mat, row, mat, row,
        ),
        check_vma=False,
    )
```

profile of v0, /device:TPU:0, one launch (start us, length us, event | category | flops | bytes accessed | tf_op | source)
XLA Modules:
  0.0 291.6 jit_solution(16203758879881919761)
XLA Ops:
  5.8 2.2 copy.61.x_ref
  17.8 2.0 broadcast_select_fusion.2
  22.0 14.8 %layer_forward.2 = (bf16[2,196,512]{2,1,0:T(8,128)(2,1)S(1)}, bf16[512,512]{1,0:T(8,128)(2,1)S(1)}, bf16[512,512]{1,0:T(8,128)(2,1)S(1)}, bf16[512,1536]{1,0:T(8...) custom-call(s32[2]{0:T(128)S(1)} %get-tuple-element.389.base_ref, ...), custom_call_target="tpu_custom_call" | custom-call | flops 12999999488 | bytes 1000000 | tf_op jit(solution)/shard_map/layer_forward/pallas_call | solution.py:412
  36.8 13.4 %layer_forward.3 = (bf16[2,196,512]{2,1,0:T(8,128)(2,1)S(1)}, bf16[512,512]{1,0:T(8,128)(2,1)S(1)}, bf16[512,512]{1,0:T(8,128)(2,1)S(1)}, bf16[512,1536]{1,0:T(8...) custom-call(s32[2]{0:T(128)S(1)} %get-tuple-element.390.base_ref, ...), custom_call_target="tpu_custom_call" | custom-call | flops 12999999488 | bytes 1000000 | tf_op jit(solution)/shard_map/layer_forward/pallas_call | solution.py:412
  50.2 8.5 %ffn_back.2 = (f32[512,512]{1,0:T(8,128)S(1)}, bf16[512,512]{1,0:T(8,128)(2,1)S(1)}, bf16[2304,512]{1,0:T(8,128)(2,1)S(1)}, bf16[2304,512]{1,0:T(8,128)(2,1)}, f32[16,512]{1,0:T(8,128)S(1)}) custom-call(s32[2]{0:T(128)S(1)} %get-tuple-element.389.base_ref, bf16[4,196,512]{2,1,0:T(8,128)(2,1)S(1)} %copy.63.g_ref, f32[2]{0:T(128)S(1)} %compare_convert_fusion.live_ref, ...), custom_call_target="tpu_custom_call" | custom-call | flops 8999999488 | bytes 1000000 | tf_op jit(solution)/shard_map/ffn_back/pallas_call | solution.py:436
  58.7 12.6 %attn_back.2 = (f32[2,196,512]{2,1,0:T(8,128)S(1)}, bf16[2,196,512]{2,1,0:T(8,128)(2,1)S(1)}, bf16[768,512]{1,0:T(8,128)(2,1)S(1)}, bf16[768,512]{1,0:T(8,128)(2...) custom-call(s32[2]{0:T(128)S(1)} %get-tuple-element.389.base_ref, bf16[256,196]{1,0:T(8,128)(2,1)S(1)} %copy-done.45, ...), custom_call_target="tpu_custom_call" | custom-call | flops 12999999488 | bytes 1000000 | tf_op jit(solution)/shard_map/attn_back/pallas_call | solution.py:465
  72.6 20.6 %ffn_back.3 = (f32[512,512]{1,0:T(8,128)S(1)}, bf16[512,512]{1,0:T(8,128)(2,1)S(1)}, bf16[2304,512]{1,0:T(8,128)(2,1)S(1)}, bf16[2304,512]{1,0:T(8,128)(2,1)}, f32[16,512]{1,0:T(8,128)S(1)}) custom-call(s32[2]{0:T(128)S(1)} %get-tuple-element.390.base_ref, bf16[2,196,512]{2,1,0:T(8,128)(2,1)S(1)} %get-tuple-element.176.g_ref, ...), custom_call_target="tpu_custom_call" | custom-call | flops 8999999488 | bytes 1000000 | tf_op jit(solution)/shard_map/ffn_back/pallas_call | solution.py:436
  94.3 12.5 %attn_back.3 = (f32[2,196,512]{2,1,0:T(8,128)S(1)}, bf16[2,196,512]{2,1,0:T(8,128)(2,1)}, bf16[768,512]{1,0:T(8,128)(2,1)S(1)}, bf16[768,512]{1,0:T(8,128)(2,1)}...) custom-call(s32[2]{0:T(128)S(1)} %get-tuple-element.390.base_ref, bf16[256,196]{1,0:T(8,128)(2,1)S(1)} %copy-done.44, ...), custom_call_target="tpu_custom_call" | custom-call | flops 12999999488 | bytes 1000000 | tf_op jit(solution)/shard_map/attn_back/pallas_call | solution.py:465
  111.2 3.3 %shard_map.342 = (bf16[512,512]{1,0:T(8,128)(2,1)S(1)}, bf16[512,512]{1,0:T(8,128)(2,1)S(1)}, bf16[512,512]{1,0:T(8,128)(2,1)}, bf16[512,512]{1,0:T(8,128)(2,1)}, bf16[256,512]{1,0:T(8,128)(2,1)S(1)}) custom-call(s32[16]{0:T(128)S(1)} %shift-right-arithmetic_and_fusion.bit_ref, bf16[2304,512]{1,0:T(8,128)(2,1)S(1)} %copy-done.3, ...), custom_call_target="tpu_custom_call" | custom-call | tf_op jit(solution)/shard_map/pallas_call | solution.py:623
  114.5 2.9 collective-permute-start.10
  118.9 2.0 shard_map.343
  123.9 2.6 collective-permute-start.13
  126.5 2.3 shard_map.348
  129.6 2.6 shard_map.349
  136.0 2.9 collective-permute-start.31
  149.9 2.4 shard_map.344
  157.3 2.9 %collective-permute-start.17 = (bf16[128,512]{1,0:T(8,128)(2,1)}, bf16[128,512]{1,0:T(8,128)(2,1)}, u32[]{:S(2)}, u32[]{:S(2)}) collective-permute-start(bf16[128,512]{1,0:T(8,128)(2,1)} %get-tuple-element.206), channel_id=1, source_target_pairs={{0,4},{1,5},{2,6},{3,7},{4,0},{5,1},{6,2},{7,3},{8,12},{9,13},{10,... | collective-permute-start | bytes 393224 | tf_op jit(solution)/shard_map/ppermute | solution.py:633
  173.3 2.9 collective-permute-start.34
  177.5 2.1 collective-permute-start.18
  181.1 2.8 collective-permute-start.20
  188.9 3.0 %collective-permute-start.37 = (bf16[128,512]{1,0:T(8,128)(2,1)S(1)}, bf16[128,512]{1,0:T(8,128)(2,1)S(1)}, u32[]{:S(2)}, u32[]{:S(2)}) collective-permute-start(bf16[128,512]{1,0:T(8,128)(2,1)S(1)} %get-tuple-element.249), channel_id=1, source_target_pairs={{0,8},{1,9},{2,10},{3,11},{4,12},{5,13},{6,14},{7,15},{8,0},{9,1},... | collective-permute-start | bytes 393224 | tf_op jit(solution)/shard_map/ppermute | solution.py:633
  215.7 4.4 %collective-permute-done.47.refs_6_ = bf16[2,32,512]{2,1,0:T(8,128)(2,1)S(1)} collective-permute-done((bf16[2,32,512]{2,1,0:T(8,128)(2,1)S(1)}, bf16[2,32,512]{2,1,0:T(8,128)(2,1)S(1)}, u32[]{:S(2)}, u32[]{:S(2)}) %collective-permute-start.47) | collective-permute-done | bytes 65568 | tf_op jit(solution)/shard_map/ppermute | solution.py:633
  222.1 2.1 collective-permute-start.50
  226.3 6.3 %collective-permute-done.51.refs_6_ = bf16[2,64,512]{2,1,0:T(8,128)(2,1)S(1)} collective-permute-done((bf16[2,64,512]{2,1,0:T(8,128)(2,1)S(1)}, bf16[2,64,512]{2,1,0:T(8,128)(2,1)S(1)}, u32[]{:S(2)}, u32[]{:S(2)}) %collective-permute-start.51) | collective-permute-done | bytes 131104 | tf_op jit(solution)/shard_map/ppermute | solution.py:633
  234.5 2.3 collective-permute-done.50.refs_5_
  238.7 2.2 collective-permute-start.55
  241.7 8.6 %collective-permute-done.55.refs_6_ = bf16[2,128,512]{2,1,0:T(8,128)(2,1)S(1)} collective-permute-done((bf16[2,128,512]{2,1,0:T(8,128)(2,1)S(1)}, bf16[2,128,512]{2,1,0:T(8,128)(2,1)S(1)}, u32[]{:S(2)}, u32[]{:S(2)}) %collective-permute-start.55) | collective-permute-done | bytes 262176 | tf_op jit(solution)/shard_map/ppermute | solution.py:633
  250.3 2.2 collective-permute-done.56.refs_7_
  260.4 2.2 copy.69
  262.5 19.5 %collective-permute-done.59.refs_6_ = bf16[2,256,512]{2,1,0:T(8,128)(2,1)S(1)} collective-permute-done((bf16[2,256,512]{2,1,0:T(8,128)(2,1)S(1)}, bf16[2,256,512]{2,1,0:T(8,128)(2,1)S(1)}, u32[]{:S(2)}, u32[]{:S(2)}) %collective-permute-start.59) | collective-permute-done | bytes 524320 | tf_op jit(solution)/shard_map/ppermute | solution.py:633
  282.0 3.4 %collective-permute-done.60.refs_7_ = bf16[2,288,512]{2,1,0:T(8,128)(2,1)S(1)} collective-permute-done((bf16[2,288,512]{2,1,0:T(8,128)(2,1)S(1)}, bf16[2,288,512]{2,1,0:T(8,128)(2,1)S(1)}, u32[]{:S(2)}, u32[]{:S(2)}) %collective-permute-start.60) | collective-permute-done | bytes 589856 | tf_op jit(solution)/shard_map/ppermute | solution.py:633
  285.5 5.9 %shard_map.359 = (f32[2048,512]{1,0:T(8,128)}, f32[512,2048]{1,0:T(8,128)}, f32[512,512]{1,0:T(8,128)}, f32[512,1536]{1,0:T(8,128)}, f32[1,512]{1,0:T(1,128)}, /...) custom-call(s32[16]{0:T(128)S(1)} %shift-right-arithmetic_and_fusion, ...), custom_call_target="tpu_custom_call" | custom-call | tf_op jit(solution)/shard_map/pallas_call | solution.py:623
  (288 shorter events, 109.0 us)
Async XLA Ops:
  4.0 11.7 %collective-permute-start.2 = (bf16[512,1536]{1,0:T(8,128)(2,1)}, bf16[512,1536]{1,0:T(8,128)(2,1)}, u32[]{:S(2)}, u32[]{:S(2)}) collective-permute-start(bf16[512,1536]{1,0:T(8,128)(2,1)} %bitcast.77), channel_id=1, source_target_pairs={{0,16},{16,0},{1,17},{17,1},{2,18},{18,2},{3,19},{19,3},{4,20},{20... | collective-permute-start | bytes 4718600 | tf_op jit(solution)/shard_map/ppermute | solution.py:685
  4.6 13.2 %collective-permute-start.4 = (bf16[512,2048]{1,0:T(8,128)(2,1)}, bf16[512,2048]{1,0:T(8,128)(2,1)}, u32[]{:S(2)}, u32[]{:S(2)}) collective-permute-start(bf16[512,2048]{1,0:T(8,128)(2,1)} %bitcast.75), channel_id=1, source_target_pairs={{0,16},{16,0},{1,17},{17,1},{2,18},{18,2},{3,19},{19,3},{4,20},{20... | collective-permute-start | bytes 6291464 | tf_op jit(solution)/shard_map/ppermute | solution.py:685
  9.5 10.4 %collective-permute-start.5 = (bf16[2048,512]{1,0:T(8,128)(2,1)}, bf16[2048,512]{1,0:T(8,128)(2,1)}, u32[]{:S(2)}, u32[]{:S(2)}) collective-permute-start(bf16[2048,512]{1,0:T(8,128)(2,1)} %bitcast.76), channel_id=1, source_target_pairs={{0,16},{16,0},{1,17},{17,1},{2,18},{18,2},{3,19},{19,3},{4,20},{20... | collective-permute-start | bytes 6291464 | tf_op jit(solution)/shard_map/ppermute | solution.py:685
  93.8 15.8 %collective-permute-start.8 = (bf16[2304,512]{1,0:T(8,128)(2,1)}, bf16[2304,512]{1,0:T(8,128)(2,1)}, u32[]{:S(2)}, u32[]{:S(2)}) collective-permute-start(bf16[2304,512]{1,0:T(8,128)(2,1)} %get-tuple-element.187), channel_id=1, source_target_pairs={{0,16},{16,0},{1,17},{17,1},{2,18},{18,2},{3,19},{19,3},{4,20},{20... | collective-permute-start | bytes 7077896 | tf_op jit(solution)/shard_map/ppermute | solution.py:685
  94.2 29.7 %collective-permute-start.26 = (bf16[2304,512]{1,0:T(8,128)(2,1)}, bf16[2304,512]{1,0:T(8,128)(2,1)}, u32[]{:S(2)}, u32[]{:S(2)}) collective-permute-start(bf16[2304,512]{1,0:T(8,128)(2,1)} %get-tuple-element.224), channel_id=1, source_target_pairs={{0,16},{16,0},{1,17},{17,1},{2,18},{18,2},{3,19},{19,3},{4,20},{20... | collective-permute-start | bytes 7077896 | tf_op jit(solution)/shard_map/ppermute | solution.py:685
  109.4 20.1 %collective-permute-start.27 = (bf16[768,512]{1,0:T(8,128)(2,1)}, bf16[768,512]{1,0:T(8,128)(2,1)}, u32[]{:S(2)}, u32[]{:S(2)}) collective-permute-start(bf16[768,512]{1,0:T(8,128)(2,1)} %get-tuple-element.229), channel_id=1, source_target_pairs={{0,16},{16,0},{1,17},{17,1},{2,18},{18,2},{3,19},{19,3},{4,20},{20... | collective-permute-start | bytes 2359304 | tf_op jit(solution)/shard_map/ppermute | solution.py:685
  114.5 32.0 %collective-permute-start.10 = (bf16[512,512]{1,0:T(8,128)(2,1)}, bf16[512,512]{1,0:T(8,128)(2,1)}, u32[]{:S(2)}, u32[]{:S(2)}) collective-permute-start(bf16[512,512]{1,0:T(8,128)(2,1)} %get-tuple-element.195), channel_id=1, source_target_pairs={{0,1},{1,0},{2,3},{3,2},{4,5},{5,4},{6,7},{7,6},{8,9},{9,8},{10,11... | collective-permute-start | bytes 1572872 | tf_op jit(solution)/shard_map/ppermute | solution.py:633
  117.4 29.6 %collective-permute-start.11 = (bf16[512,512]{1,0:T(8,128)(2,1)}, bf16[512,512]{1,0:T(8,128)(2,1)}, u32[]{:S(2)}, u32[]{:S(2)}) collective-permute-start(bf16[512,512]{1,0:T(8,128)(2,1)} %get-tuple-element.196), channel_id=1, source_target_pairs={{0,2},{1,3},{2,0},{3,1},{4,6},{5,7},{6,4},{7,5},{8,10},{9,11},{10,... | collective-permute-start | bytes 1572872 | tf_op jit(solution)/shard_map/ppermute | solution.py:633
  122.3 13.0 %collective-permute-start.12 = (bf16[256,512]{1,0:T(8,128)(2,1)S(1)}, bf16[256,512]{1,0:T(8,128)(2,1)S(1)}, u32[]{:S(2)}, u32[]{:S(2)}) collective-permute-start(bf16[256,512]{1,0:T(8,128)(2,1)S(1)} %get-tuple-element.197), channel_id=1, source_target_pairs={{0,4},{1,5},{2,6},{3,7},{4,0},{5,1},{6,2},{7,3},{8,12},{9,13},{10,... | collective-permute-start | bytes 786440 | tf_op jit(solution)/shard_map/ppermute | solution.py:633
  123.9 22.1 %collective-permute-start.13 = (bf16[256,512]{1,0:T(8,128)(2,1)}, bf16[256,512]{1,0:T(8,128)(2,1)}, u32[]{:S(2)}, u32[]{:S(2)}) collective-permute-start(bf16[256,512]{1,0:T(8,128)(2,1)} %get-tuple-element.198), channel_id=1, source_target_pairs={{0,8},{1,9},{2,10},{3,11},{4,12},{5,13},{6,14},{7,15},{8,0},{9,1},... | collective-permute-start | bytes 786440 | tf_op jit(solution)/shard_map/ppermute | solution.py:633
  133.6 23.6 %collective-permute-start.30 = (bf16[256,512]{1,0:T(8,128)(2,1)}, bf16[256,512]{1,0:T(8,128)(2,1)}, u32[]{:S(2)}, u32[]{:S(2)}) collective-permute-start(bf16[256,512]{1,0:T(8,128)(2,1)} %get-tuple-element.234), channel_id=1, source_target_pairs={{0,4},{1,5},{2,6},{3,7},{4,0},{5,1},{6,2},{7,3},{8,12},{9,13},{10,... | collective-permute-start | bytes 786440 | tf_op jit(solution)/shard_map/ppermute | solution.py:633
  136.0 21.3 %collective-permute-start.31 = (bf16[256,512]{1,0:T(8,128)(2,1)}, bf16[256,512]{1,0:T(8,128)(2,1)}, u32[]{:S(2)}, u32[]{:S(2)}) collective-permute-start(bf16[256,512]{1,0:T(8,128)(2,1)} %get-tuple-element.235), channel_id=1, source_target_pairs={{0,8},{1,9},{2,10},{3,11},{4,12},{5,13},{6,14},{7,15},{8,0},{9,1},... | collective-permute-start | bytes 786440 | tf_op jit(solution)/shard_map/ppermute | solution.py:633
  145.9 20.9 %collective-permute-start.28 = (bf16[512,512]{1,0:T(8,128)(2,1)}, bf16[512,512]{1,0:T(8,128)(2,1)}, u32[]{:S(2)}, u32[]{:S(2)}) collective-permute-start(bf16[512,512]{1,0:T(8,128)(2,1)} %copy-done.42), channel_id=1, source_target_pairs={{0,1},{1,0},{2,3},{3,2},{4,5},{5,4},{6,7},{7,6},{8,9},{9,8},{10,11... | collective-permute-start | bytes 1572872 | tf_op jit(solution)/shard_map/ppermute | solution.py:633
  146.5 21.9 %collective-permute-start.29 = (bf16[512,512]{1,0:T(8,128)(2,1)}, bf16[512,512]{1,0:T(8,128)(2,1)}, u32[]{:S(2)}, u32[]{:S(2)}) collective-permute-start(bf16[512,512]{1,0:T(8,128)(2,1)} %copy-done.41), channel_id=1, source_target_pairs={{0,2},{1,3},{2,0},{3,1},{4,6},{5,7},{6,4},{7,5},{8,10},{9,11},{10,... | collective-permute-start | bytes 1572872 | tf_op jit(solution)/shard_map/ppermute | solution.py:633
  155.7 20.4 %collective-permute-start.14 = (bf16[256,512]{1,0:T(8,128)(2,1)}, bf16[256,512]{1,0:T(8,128)(2,1)}, u32[]{:S(2)}, u32[]{:S(2)}) collective-permute-start(bf16[256,512]{1,0:T(8,128)(2,1)} %get-tuple-element.203), channel_id=1, source_target_pairs={{0,2},{1,3},{2,0},{3,1},{4,6},{5,7},{6,4},{7,5},{8,10},{9,11},{10,... | collective-permute-start | bytes 786440 | tf_op jit(solution)/shard_map/ppermute | solution.py:633
  157.2 15.5 %collective-permute-start.16 = (bf16[128,512]{1,0:T(8,128)(2,1)}, bf16[128,512]{1,0:T(8,128)(2,1)}, u32[]{:S(2)}, u32[]{:S(2)}) collective-permute-start(bf16[128,512]{1,0:T(8,128)(2,1)} %get-tuple-element.205), channel_id=1, source_target_pairs={{0,8},{1,9},{2,10},{3,11},{4,12},{5,13},{6,14},{7,15},{8,0},{9,1},... | collective-permute-start | bytes 393224 | tf_op jit(solution)/shard_map/ppermute | solution.py:633
  157.3 16.0 %collective-permute-start.17 = (bf16[128,512]{1,0:T(8,128)(2,1)}, bf16[128,512]{1,0:T(8,128)(2,1)}, u32[]{:S(2)}, u32[]{:S(2)}) collective-permute-start(bf16[128,512]{1,0:T(8,128)(2,1)} %get-tuple-element.206), channel_id=1, source_target_pairs={{0,4},{1,5},{2,6},{3,7},{4,0},{5,1},{6,2},{7,3},{8,12},{9,13},{10,... | collective-permute-start | bytes 393224 | tf_op jit(solution)/shard_map/ppermute | solution.py:633
  172.2 15.8 %collective-permute-start.32 = (bf16[256,512]{1,0:T(8,128)(2,1)S(1)}, bf16[256,512]{1,0:T(8,128)(2,1)S(1)}, u32[]{:S(2)}, u32[]{:S(2)}) collective-permute-start(bf16[256,512]{1,0:T(8,128)(2,1)S(1)} %get-tuple-element.240), channel_id=1, source_target_pairs={{0,2},{1,3},{2,0},{3,1},{4,6},{5,7},{6,4},{7,5},{8,10},{9,11},{10,... | collective-permute-start | bytes 786440 | tf_op jit(solution)/shard_map/ppermute | solution.py:633
  172.7 15.3 %collective-permute-start.33 = (bf16[256,512]{1,0:T(8,128)(2,1)S(1)}, bf16[256,512]{1,0:T(8,128)(2,1)S(1)}, u32[]{:S(2)}, u32[]{:S(2)}) collective-permute-start(bf16[256,512]{1,0:T(8,128)(2,1)S(1)} %get-tuple-element.241), channel_id=1, source_target_pairs={{0,1},{1,0},{2,3},{3,2},{4,5},{5,4},{6,7},{7,6},{8,9},{9,8},{10,11... | collective-permute-start | bytes 786440 | tf_op jit(solution)/shard_map/ppermute | solution.py:633
  177.5 14.7 %collective-permute-start.18 = (bf16[128,512]{1,0:T(8,128)(2,1)S(1)}, bf16[128,512]{1,0:T(8,128)(2,1)S(1)}, u32[]{:S(2)}, u32[]{:S(2)}) collective-permute-start(bf16[128,512]{1,0:T(8,128)(2,1)S(1)} %get-tuple-element.211), channel_id=1, source_target_pairs={{0,4},{1,5},{2,6},{3,7},{4,0},{5,1},{6,2},{7,3},{8,12},{9,13},{10,... | collective-permute-start | bytes 393224 | tf_op jit(solution)/shard_map/ppermute | solution.py:633
  188.9 11.4 %collective-permute-start.37 = (bf16[128,512]{1,0:T(8,128)(2,1)S(1)}, bf16[128,512]{1,0:T(8,128)(2,1)S(1)}, u32[]{:S(2)}, u32[]{:S(2)}) collective-permute-start(bf16[128,512]{1,0:T(8,128)(2,1)S(1)} %get-tuple-element.249), channel_id=1, source_target_pairs={{0,8},{1,9},{2,10},{3,11},{4,12},{5,13},{6,14},{7,15},{8,0},{9,1},... | collective-permute-start | bytes 393224 | tf_op jit(solution)/shard_map/ppermute | solution.py:633
  222.0 12.4 %collective-permute-start.49 = (bf16[2,128,512]{2,1,0:T(8,128)(2,1)S(1)}, bf16[2,128,512]{2,1,0:T(8,128)(2,1)S(1)}, u32[]{:S(2)}, u32[]{:S(2)}) collective-permute-start(bf16[2,128,512]{2,1,0:T(8,128)(2,1)S(1)} %get-tuple-element.276.refs_0_), channel_id=1, source_target_pairs={{0,4},{1,5},{2,6},{3,7},{4,0},{5,1},{6,2},{7,3},{8,12},{9,13},{10,... | collective-permute-start | bytes 786440 | tf_op jit(solution)/shard_map/ppermute | solution.py:633
  222.1 14.7 %collective-permute-start.50 = (bf16[2,128,512]{2,1,0:T(8,128)(2,1)S(1)}, bf16[2,128,512]{2,1,0:T(8,128)(2,1)S(1)}, u32[]{:S(2)}, u32[]{:S(2)}) collective-permute-start(bf16[2,128,512]{2,1,0:T(8,128)(2,1)S(1)} %get-tuple-element.277.refs_1_), channel_id=1, source_target_pairs={{0,8},{1,9},{2,10},{3,11},{4,12},{5,13},{6,14},{7,15},{8,0},{9,1},... | collective-permute-start | bytes 786440 | tf_op jit(solution)/shard_map/ppermute | solution.py:633
  237.5 15.1 %collective-permute-start.53 = (bf16[2,256,512]{2,1,0:T(8,128)(2,1)S(1)}, bf16[2,256,512]{2,1,0:T(8,128)(2,1)S(1)}, u32[]{:S(2)}, u32[]{:S(2)}) collective-permute-start(bf16[2,256,512]{2,1,0:T(8,128)(2,1)S(1)} %get-tuple-element.280.refs_0_), channel_id=1, source_target_pairs={{0,2},{1,3},{2,0},{3,1},{4,6},{5,7},{6,4},{7,5},{8,10},{9,11},{10,... | collective-permute-start | bytes 1572872 | tf_op jit(solution)/shard_map/ppermute | solution.py:633
  238.1 14.5 %collective-permute-start.54 = (bf16[2,256,512]{2,1,0:T(8,128)(2,1)S(1)}, bf16[2,256,512]{2,1,0:T(8,128)(2,1)S(1)}, u32[]{:S(2)}, u32[]{:S(2)}) collective-permute-start(bf16[2,256,512]{2,1,0:T(8,128)(2,1)S(1)} %get-tuple-element.281.refs_1_), channel_id=1, source_target_pairs={{0,1},{1,0},{2,3},{3,2},{4,5},{5,4},{6,7},{7,6},{8,9},{9,8},{10,11... | collective-permute-start | bytes 1572872 | tf_op jit(solution)/shard_map/ppermute | solution.py:633
  238.7 13.9 %collective-permute-start.56 = (bf16[2,160,512]{2,1,0:T(8,128)(2,1)S(1)}, bf16[2,160,512]{2,1,0:T(8,128)(2,1)S(1)}, u32[]{:S(2)}, u32[]{:S(2)}) collective-permute-start(bf16[2,160,512]{2,1,0:T(8,128)(2,1)S(1)} %get-tuple-element.283.refs_3_), channel_id=1, source_target_pairs={{0,4},{1,5},{2,6},{3,7},{4,0},{5,1},{6,2},{7,3},{8,12},{9,13},{10,... | collective-permute-start | bytes 983048 | tf_op jit(solution)/shard_map/ppermute | solution.py:633
  238.7 11.6 %collective-permute-start.55 = (bf16[2,128,512]{2,1,0:T(8,128)(2,1)S(1)}, bf16[2,128,512]{2,1,0:T(8,128)(2,1)S(1)}, u32[]{:S(2)}, u32[]{:S(2)}) collective-permute-start(bf16[2,128,512]{2,1,0:T(8,128)(2,1)S(1)} %get-tuple-element.282.refs_2_), channel_id=1, source_target_pairs={{0,8},{1,9},{2,10},{3,11},{4,12},{5,13},{6,14},{7,15},{8,0},{9,1},... | collective-permute-start | bytes 786440 | tf_op jit(solution)/shard_map/ppermute | solution.py:633
  241.6 18.3 %collective-permute-start.7 = (f32[2,196,512]{2,0,1:T(2,128)S(1)}, f32[2,196,512]{2,0,1:T(2,128)S(1)}, u32[]{:S(2)}, u32[]{:S(2)}) collective-permute-start(f32[2,196,512]{2,0,1:T(2,128)S(1)} %copy.64), channel_id=1, source_target_pairs={{0,16},{16,0},{1,17},{17,1},{2,18},{18,2},{3,19},{19,3},{4,20},{20... | collective-permute-start | bytes 2408456 | tf_op jit(solution)/shard_map/ppermute | solution.py:685
  253.3 32.2 %collective-permute-start.57 = (bf16[2,512,512]{2,1,0:T(8,128)(2,1)S(1)}, bf16[2,512,512]{2,1,0:T(8,128)(2,1)S(1)}, u32[]{:S(2)}, u32[]{:S(2)}) collective-permute-start(bf16[2,512,512]{2,1,0:T(8,128)(2,1)S(1)} %get-tuple-element.284.refs_0_), channel_id=1, source_target_pairs={{0,1},{1,0},{2,3},{3,2},{4,5},{5,4},{6,7},{7,6},{8,9},{9,8},{10,11... | collective-permute-start | bytes 3145736 | tf_op jit(solution)/shard_map/ppermute | solution.py:633
  254.7 30.8 %collective-permute-start.58 = (bf16[2,512,512]{2,1,0:T(8,128)(2,1)S(1)}, bf16[2,512,512]{2,1,0:T(8,128)(2,1)S(1)}, u32[]{:S(2)}, u32[]{:S(2)}) collective-permute-start(bf16[2,512,512]{2,1,0:T(8,128)(2,1)S(1)} %get-tuple-element.285.refs_1_), channel_id=1, source_target_pairs={{0,2},{1,3},{2,0},{3,1},{4,6},{5,7},{6,4},{7,5},{8,10},{9,11},{10,... | collective-permute-start | bytes 3145736 | tf_op jit(solution)/shard_map/ppermute | solution.py:633
  256.3 29.2 %collective-permute-start.60 = (bf16[2,288,512]{2,1,0:T(8,128)(2,1)S(1)}, bf16[2,288,512]{2,1,0:T(8,128)(2,1)S(1)}, u32[]{:S(2)}, u32[]{:S(2)}) collective-permute-start(bf16[2,288,512]{2,1,0:T(8,128)(2,1)S(1)} %get-tuple-element.287.refs_3_), channel_id=1, source_target_pairs={{0,8},{1,9},{2,10},{3,11},{4,12},{5,13},{6,14},{7,15},{8,0},{9,1},... | collective-permute-start | bytes 1769480 | tf_op jit(solution)/shard_map/ppermute | solution.py:633
  258.0 24.0 %collective-permute-start.59 = (bf16[2,256,512]{2,1,0:T(8,128)(2,1)S(1)}, bf16[2,256,512]{2,1,0:T(8,128)(2,1)S(1)}, u32[]{:S(2)}, u32[]{:S(2)}) collective-permute-start(bf16[2,256,512]{2,1,0:T(8,128)(2,1)S(1)} %get-tuple-element.286.refs_2_), channel_id=1, source_target_pairs={{0,4},{1,5},{2,6},{3,7},{4,0},{5,1},{6,2},{7,3},{8,12},{9,13},{10,... | collective-permute-start | bytes 1572872 | tf_op jit(solution)/shard_map/ppermute | solution.py:633
  (91 other events, 611.6 us)
where the time goes:
time: 297 us; the launch traced here: 292 us
  Pallas kernels  109 us (37%)
  starting transfers between devices  62.8 us (21%)
  waiting for transfers between devices  60.4 us (20%)
  local copies, waits for them, and re-layouts  42.4 us (14%)
  other arithmetic  12.5 us (4%)
    ppermute x48, starting transfers between devices, exchange(): lax.ppermute(value, 'dp', [(one, one ^ 1 << bit) for one in range(count)])  59.8 us
    ppermute x48, waiting for transfers between devices, exchange(): lax.ppermute(value, 'dp', [(one, one ^ 1 << bit) for one in range(count)])  58.4 us
    pallas_call x2, Pallas kernels, run_ffn_back(): pl.pallas_call(functools.partial(ffn_back_kernel, images=images), out_sha...  29.1 us
    pallas_call x2, Pallas kernels, run_forward(): pl.pallas_call(functools.partial(forward_kernel, images=images, head_dim=...  28.2 us
    pallas_call x18, Pallas kernels, small_call(): pl.pallas_call(functools.partial(kernel, turn=4 * turn), out_shape=tuple(...  26.8 us
    unnamed x129, local copies, waits for them, and re-layouts  25.2 us
    pallas_call x2, Pallas kernels, run_attn_back(): pl.pallas_call(functools.partial(attn_back_kernel, images=images, head_di...  25.1 us
    select_n x5, other arithmetic, both(): second = jnp.where(section == 0, other, value)  7.08 us
  transfers between devices with their start and end apart: 61, of which 17 were waited for; matrix products, arithmetic and copies ran while one was open for 12% of the time, Pallas kernels for 11%

commit v1 on v0

--- a/solution.py
+++ b/solution.py
@@ -248,14 +248,28 @@
     base_ref, g_ref, live_ref, perm_ref, vec_ref, wout_ref, wup_ref, wdown_ref,
     mix_ref, res_ref, n2_ref, act_ref, slope_ref,
     dres_ref, dmix_ref, keep_ref, send_ref,
-    small_ref, gb_ref, dpre_ref, dresb_ref,
-    *, images,
+    small_ref, gb_ref, dpre_ref, dresb_ref, *local,
+    images,
 ):
+    fetches = ()
+    if local:
+        *local, sem = local
+        sources = (mix_ref, res_ref, n2_ref, act_ref, slope_ref)
+        fetches = [
+            pltpu.make_async_copy(source, dest, sem.at[number])
+            for number, (source, dest) in enumerate(zip(sources, local))
+        ]
+        for fetch in reversed(fetches):
+            fetch.start()
+        mix_ref, res_ref, n2_ref, act_ref, slope_ref = local
     width = wout_ref.shape[0]
     hidden = wup_ref.shape[1]
     first = base_ref[0]
     section = base_ref[1]
     small_ref[...] = jnp.zeros_like(small_ref)
+    if fetches:
+        fetches[4].wait()
+        fetches[1].wait()
 
     def step(img, carry):
         rows = rows_at(img, IROWS)
@@ -281,6 +295,8 @@
 
     lax.fori_loop(0, images, step, 0)
     span = hidden // 2
+    for fetch in (fetches[0], fetches[2], fetches[3]) if fetches else ():
+        fetch.wait()
     for side, dest in ((0, keep_ref), (1, send_ref)):
         half = section if side == 0 else 1 - section
 
@@ -369,6 +385,10 @@
 
 def vmem():
     return pl.BlockSpec(memory_space=pltpu.VMEM)
+
+
+def hbm():
+    return pl.BlockSpec(memory_space=pltpu.HBM)
 
 
 def smem():
@@ -411,9 +431,9 @@
         scratch += [pltpu.SemaphoreType.DMA((5,)), pltpu.SemaphoreType.DMA((9, images))]
     return pl.pallas_call(
         functools.partial(forward_kernel, images=images, head_dim=head_dim, masked=masked, spill=spill),
-        out_shape=shapes,
+        out_shape=(shapes[0], *(pltpu.HBM(part.shape, part.dtype) if spill else part for part in shapes[1:])),
         in_specs=[smem()] + [vmem()] * 8,
-        out_specs=(vmem(), *(pl.BlockSpec(memory_space=pl.ANY) if spill else vmem() for _ in shapes[1:])),
+        out_specs=(vmem(), *(hbm() if spill else vmem() for _ in shapes[1:])),
         scratch_shapes=scratch,
         compiler_params=SPILL_PARAMS if spill else PARAMS,
         cost_estimate=busy(13),
@@ -421,7 +441,7 @@
     )(base, rows_in, perm, bias, vec, wqkv, wout, wup, wdown)
 
 
-def run_ffn_back(base, g_rows, live, perm, vec, weights, kept, images):
+def run_ffn_back(base, g_rows, live, perm, vec, weights, kept, images, fetch):
     _, wout, wup, wdown = weights
     _, _, _, _, mix, res, n2, act, slope = kept
     width, hidden = wup.shape
@@ -433,16 +453,20 @@
         shape_of((hidden + width // 2, width), BF16),
         shape_of((SMALL_ROWS, width), F32),
     )
+    scratch = []
+    if fetch:
+        scratch = [pltpu.VMEM(part.shape, part.dtype) for part in (mix, res, n2, act, slope)]
+        scratch.append(pltpu.SemaphoreType.DMA((5,)))
     return pl.pallas_call(
         functools.partial(ffn_back_kernel, images=images),
         out_shape=shapes,
-        in_specs=[smem(), vmem(), smem()] + [vmem()] * 10,
+        in_specs=[smem(), vmem(), smem()] + [vmem()] * 5 + [hbm() if fetch else vmem()] * 5,
         out_specs=tuple(vmem() for _ in shapes),
         scratch_shapes=[
             pltpu.VMEM((total, width), BF16),
             pltpu.VMEM((total, hidden), BF16),
             pltpu.VMEM((total, width), BF16),
-        ],
+        ] + scratch,
         compiler_params=PARAMS,
         cost_estimate=busy(9),
         name="ffn_back",
@@ -669,7 +693,9 @@
     parts = small_call(join_kernel, where, (own, got), shapes)
     rounds = len(orders[0])
     for turn in reversed(range(rounds)):
-        recv = [exchange(part, order[turn], count) for part, order in zip(parts, orders)]
+        recv = []
+        for part, order in zip(parts, orders):
+            recv.append(exchange(part, order[turn], count))
         if turn:
             shapes = [
                 shape_of((2, 2 * part.shape[1] - extra, width), BF16) for part, extra in zip(parts, extras)
@@ -683,6 +709,43 @@
 
 def swap(value):
     return lax.ppermute(value, "section", [(0, 1), (1, 0)])
+
+
+def weights_kernel(section_ref, *refs):
+    own, got, zero, one, sem = refs[:4], refs[4:8], refs[8:12], refs[12:16], refs[16]
+
+    def copy_all(first, second):
+        copies = [
+            pltpu.make_async_copy(source, dest, sem.at[number])
+            for number, (source, dest) in enumerate(zip((*first, *second), (*zero, *one)))
+        ]
+        for copy in copies:
+            copy.start()
+        for copy in copies:
+            copy.wait()
+
+    @pl.when(section_ref[0] == 0)
+    def _():
+        copy_all(own, got)
+
+    @pl.when(section_ref[0] != 0)
+    def _():
+        copy_all(got, own)
+
+
+def both_weights(weights, where):
+    got = [swap(weight) for weight in weights]
+    shapes = [shape_of(weight.shape, weight.dtype) for weight in weights] * 2
+    picked = pl.pallas_call(
+        weights_kernel,
+        out_shape=tuple(shapes),
+        in_specs=[smem()] + [pl.BlockSpec(memory_space=pl.ANY)] * 8,
+        out_specs=tuple(vmem() for _ in shapes),
+        scratch_shapes=[pltpu.SemaphoreType.DMA((8,))],
+        compiler_params=SMALL_PARAMS,
+        name="pick_weights",
+    )(where, *weights, *got)
+    return picked[:4], picked[4:]
 
 
 def both(value, section):
@@ -722,7 +785,8 @@
          up_bias.reshape(-1, width)], axis=0)
     layer_vec = both(vectors, section)
     layer_table = both(bias_table[0], section)
-    layer_w = list(zip(*[both(weight[0], section) for weight in (qkv_weight, out_weight, up_weight, down_weight)]))
+    where = section.astype(jnp.int32).reshape(1)
+    layer_w = both_weights([weight[0] for weight in (qkv_weight, out_weight, up_weight, down_weight)], where)
     perms = [jnp.asarray(window_onehot(shift), BF16) for shift in (0, SHIFT)]
     onehot = pair_onehot()
     biases = bias_tiles(jnp.stack(layer_table), onehot)
@@ -742,7 +806,7 @@
 
     def backward(layer, base, g_rows, alive, kept):
         dres, dmix, keep_ffn, send_ffn, small_ffn = run_ffn_back(
-            base, g_rows, alive, perms[layer], layer_vec[layer], layer_w[layer], kept, mine)
+            base, g_rows, alive, perms[layer], layer_vec[layer], layer_w[layer], kept, mine, layer == 0)
         igrad, igrad_b, keep_qkv, send_qkv, tiles, small_attn = run_attn_back(
             base, perms[layer], layer_vec[layer], layer_w[layer], kept, dres, dmix, mine, head_dim)
         parts = start_rounds(keep_ffn, send_ffn, keep_qkv, send_qkv, place_bits)
@@ -762,7 +826,6 @@
 
     hidden = up_bias.shape[1]
     sizes = [half >> (bits - 1) for half in halves]
-    where = section.astype(jnp.int32).reshape(1)
     g_down, g_up, g_out, g_qkv, *vecs, g_up_b, g_table = gather_layer(
         shard_zero, shard_one, small_zero, small_one, where, sizes, hidden, bias_table.shape[1], heads, orders,
         place_bits, count)

time: 297 us -> 300 us (1.010)
  other arithmetic: 12.5 us -> 6.32 us
  Pallas kernels: 109 us -> 114 us
  local copies, waits for them, and re-layouts: 42.4 us -> 46.8 us
    select_n x5 -> x1, other arithmetic: 7.08 us -> 0.8 us  [both(): second = jnp.where(section == 0, other, value)]
    pallas_call x0 -> x1, Pallas kernels: none -> 3.36 us  [both_weights(): pl.pallas_call(weights_kernel, out_shape=tuple(shapes), in_specs=[smem()]...]
    unnamed x129 -> x149, local copies, waits for them, and re-layouts: 25.2 us -> 25.3 us
  transfers between devices with their start and end apart: 61 -> 61, of which waited for: 17 -> 17; matrix products, arithmetic and copies ran while one was open for 12% -> 13% of each run, Pallas kernels for 11% -> 11%
where the time goes in v1:
time: 300 us; the launch traced here: 295 us
  Pallas kernels  114 us (38%)
  starting transfers between devices  62.5 us (21%)
  waiting for transfers between devices  61.7 us (21%)
  local copies, waits for them, and re-layouts  46.8 us (16%)
  other arithmetic  6.32 us (2%)
    ppermute x48, waiting for transfers between devices, exchange(): lax.ppermute(value, 'dp', [(one, one ^ 1 << bit) for one in range(count)])  59.6 us
    ppermute x48, starting transfers between devices, exchange(): lax.ppermute(value, 'dp', [(one, one ^ 1 << bit) for one in range(count)])  59.5 us
    pallas_call x2, Pallas kernels, run_ffn_back(): pl.pallas_call(functools.partial(ffn_back_kernel, images=images), out_sha...  29.5 us
    pallas_call x2, Pallas kernels, run_forward(): pl.pallas_call(functools.partial(forward_kernel, images=images, head_dim=...  28.9 us
    pallas_call x18, Pallas kernels, small_call(): pl.pallas_call(functools.partial(kernel, turn=4 * turn), out_shape=tuple(...  26.8 us
    unnamed x149, local copies, waits for them, and re-layouts  25.3 us
    pallas_call x2, Pallas kernels, run_attn_back(): pl.pallas_call(functools.partial(attn_back_kernel, images=images, head_di...  25.1 us
  transfers between devices with their start and end apart: 61, of which 17 were waited for; matrix products, arithmetic and copies ran while one was open for 13% of the time, Pallas kernels for 11%

profile of v1, /device:TPU:0, one launch (start us, length us, event | category | flops | bytes accessed | tf_op | source)
XLA Modules:
  0.0 295.3 jit_solution(16546695222141956723)
XLA Ops:
  5.8 2.2 copy.61.x_ref
  15.9 2.2 copy.60
  23.4 3.4 %pick_weights.1 = (bf16[512,1536]{1,0:T(8,128)(2,1)S(1)}, bf16[512,512]{1,0:T(8,128)(2,1)S(1)}, bf16[512,2048]{1,0:T(8,128)(2,1)S(1)}, bf16[2048,512]{1,0:T(8,12...) custom-call(s32[1]{0:T(128)} %bitcast.1.section_ref, ...), custom_call_target="tpu_custom_call" | custom-call | tf_op jit(solution)/shard_map/pick_weights/pallas_call | solution.py:739
  26.8 15.4 %layer_forward.2 = (bf16[2,196,512]{2,1,0:T(8,128)(2,1)S(1)}, bf16[512,512]{1,0:T(8,128)(2,1)}, bf16[512,512]{1,0:T(8,128)(2,1)}, bf16[512,1536]{1,0:T(8,128)(2,...) custom-call(s32[2]{0:T(128)S(1)} %get-tuple-element.397.base_ref, ...), custom_call_target="tpu_custom_call" | custom-call | flops 12999999488 | bytes 1000000 | tf_op jit(solution)/shard_map/layer_forward/pallas_call | solution.py:432
  42.2 13.5 %layer_forward.3 = (bf16[2,196,512]{2,1,0:T(8,128)(2,1)S(1)}, bf16[512,512]{1,0:T(8,128)(2,1)S(1)}, bf16[512,512]{1,0:T(8,128)(2,1)S(1)}, bf16[512,1536]{1,0:T(8...) custom-call(s32[2]{0:T(128)S(1)} %get-tuple-element.398.base_ref, ...), custom_call_target="tpu_custom_call" | custom-call | flops 12999999488 | bytes 1000000 | tf_op jit(solution)/shard_map/layer_forward/pallas_call | solution.py:432
  55.8 8.5 %ffn_back.2 = (f32[512,512]{1,0:T(8,128)S(1)}, bf16[512,512]{1,0:T(8,128)(2,1)S(1)}, bf16[2304,512]{1,0:T(8,128)(2,1)S(1)}, bf16[2304,512]{1,0:T(8,128)(2,1)}, f32[16,512]{1,0:T(8,128)S(1)}) custom-call(s32[2]{0:T(128)S(1)} %get-tuple-element.397.base_ref, bf16[4,196,512]{2,1,0:T(8,128)(2,1)S(1)} %copy-done.7, f32[2]{0:T(128)S(1)} %compare_convert_fusion.live_ref, ...), custom_call_target="tpu_custom_call" | custom-call | flops 8999999488 | bytes 1000000 | tf_op jit(solution)/shard_map/ffn_back/pallas_call | solution.py:460
  64.3 12.6 %attn_back.2 = (f32[2,196,512]{2,1,0:T(8,128)S(1)}, bf16[2,196,512]{2,1,0:T(8,128)(2,1)S(1)}, bf16[768,512]{1,0:T(8,128)(2,1)S(1)}, bf16[768,512]{1,0:T(8,128)(2...) custom-call(s32[2]{0:T(128)S(1)} %get-tuple-element.397.base_ref, bf16[256,196]{1,0:T(8,128)(2,1)S(1)} %copy-done.49, ...), custom_call_target="tpu_custom_call" | custom-call | flops 12999999488 | bytes 1000000 | tf_op jit(solution)/shard_map/attn_back/pallas_call | solution.py:489
  77.6 21.0 %ffn_back.3 = (f32[512,512]{1,0:T(8,128)S(1)}, bf16[512,512]{1,0:T(8,128)(2,1)S(1)}, bf16[2304,512]{1,0:T(8,128)(2,1)S(1)}, bf16[2304,512]{1,0:T(8,128)(2,1)}, f32[16,512]{1,0:T(8,128)S(1)}) custom-call(s32[2]{0:T(128)S(1)} %get-tuple-element.398.base_ref, bf16[2,196,512]{2,1,0:T(8,128)(2,1)S(1)} %get-tuple-element.192.g_ref, ...), custom_call_target="tpu_custom_call" | custom-call | flops 8999999488 | bytes 1000000 | tf_op jit(solution)/shard_map/ffn_back/pallas_call | solution.py:460
  99.3 12.6 %attn_back.3 = (f32[2,196,512]{2,1,0:T(8,128)S(1)}, bf16[2,196,512]{2,1,0:T(8,128)(2,1)}, bf16[768,512]{1,0:T(8,128)(2,1)S(1)}, bf16[768,512]{1,0:T(8,128)(2,1)}...) custom-call(s32[2]{0:T(128)S(1)} %get-tuple-element.398.base_ref, bf16[256,196]{1,0:T(8,128)(2,1)S(1)} %copy-done.48, ...), custom_call_target="tpu_custom_call" | custom-call | flops 12999999488 | bytes 1000000 | tf_op jit(solution)/shard_map/attn_back/pallas_call | solution.py:489
  115.6 3.3 %shard_map.342 = (bf16[512,512]{1,0:T(8,128)(2,1)S(1)}, bf16[512,512]{1,0:T(8,128)(2,1)S(1)}, bf16[512,512]{1,0:T(8,128)(2,1)}, bf16[512,512]{1,0:T(8,128)(2,1)}, bf16[256,512]{1,0:T(8,128)(2,1)S(1)}) custom-call(s32[16]{0:T(128)S(1)} %shift-right-arithmetic_and_fusion.bit_ref, bf16[2304,512]{1,0:T(8,128)(2,1)S(1)} %copy-done.3, ...), custom_call_target="tpu_custom_call" | custom-call | tf_op jit(solution)/shard_map/pallas_call | solution.py:647
  118.9 3.0 %collective-permute-start.10 = (bf16[512,512]{1,0:T(8,128)(2,1)}, bf16[512,512]{1,0:T(8,128)(2,1)}, u32[]{:S(2)}, u32[]{:S(2)}) collective-permute-start(bf16[512,512]{1,0:T(8,128)(2,1)} %get-tuple-element.211), channel_id=1, source_target_pairs={{0,1},{1,0},{2,3},{3,2},{4,5},{5,4},{6,7},{7,6},{8,9},{9,8},{10,11... | collective-permute-start | bytes 1572872 | tf_op jit(solution)/shard_map/ppermute | solution.py:657
  127.7 2.6 collective-permute-start.13
  130.3 2.2 shard_map.348
  132.6 2.7 shard_map.349
  137.1 2.7 collective-permute-done.12.refs_6_
  140.5 2.1 collective-permute-start.31
  153.6 2.3 shard_map.344
  161.7 2.2 collective-permute-start.17
  176.9 2.9 collective-permute-start.34
  184.6 3.0 %collective-permute-start.20 = (bf16[64,512]{1,0:T(8,128)(2,1)S(1)}, bf16[64,512]{1,0:T(8,128)(2,1)S(1)}, u32[]{:S(2)}, u32[]{:S(2)}) collective-permute-start(bf16[64,512]{1,0:T(8,128)(2,1)S(1)} %get-tuple-element.229), channel_id=1, source_target_pairs={{0,1},{1,0},{2,3},{3,2},{4,5},{5,4},{6,7},{7,6},{8,9},{9,8},{10,11... | collective-permute-start | bytes 196616 | tf_op jit(solution)/shard_map/ppermute | solution.py:657
  192.6 3.0 collective-permute-start.37
  219.5 4.4 %collective-permute-done.47.refs_6_ = bf16[2,32,512]{2,1,0:T(8,128)(2,1)S(1)} collective-permute-done((bf16[2,32,512]{2,1,0:T(8,128)(2,1)S(1)}, bf16[2,32,512]{2,1,0:T(8,128)(2,1)S(1)}, u32[]{:S(2)}, u32[]{:S(2)}) %collective-permute-start.47) | collective-permute-done | bytes 65568 | tf_op jit(solution)/shard_map/ppermute | solution.py:657
  225.8 2.2 collective-permute-start.50
  230.0 6.3 %collective-permute-done.51.refs_6_ = bf16[2,64,512]{2,1,0:T(8,128)(2,1)S(1)} collective-permute-done((bf16[2,64,512]{2,1,0:T(8,128)(2,1)S(1)}, bf16[2,64,512]{2,1,0:T(8,128)(2,1)S(1)}, u32[]{:S(2)}, u32[]{:S(2)}) %collective-permute-start.51) | collective-permute-done | bytes 131104 | tf_op jit(solution)/shard_map/ppermute | solution.py:657
  238.2 2.3 collective-permute-done.50.refs_5_
  242.3 2.3 collective-permute-start.55
  245.4 8.5 %collective-permute-done.55.refs_6_ = bf16[2,128,512]{2,1,0:T(8,128)(2,1)S(1)} collective-permute-done((bf16[2,128,512]{2,1,0:T(8,128)(2,1)S(1)}, bf16[2,128,512]{2,1,0:T(8,128)(2,1)S(1)}, u32[]{:S(2)}, u32[]{:S(2)}) %collective-permute-start.55) | collective-permute-done | bytes 262176 | tf_op jit(solution)/shard_map/ppermute | solution.py:657
  253.9 2.2 collective-permute-done.56.refs_7_
  264.1 2.2 copy.69
  266.3 19.5 %collective-permute-done.59.refs_6_ = bf16[2,256,512]{2,1,0:T(8,128)(2,1)S(1)} collective-permute-done((bf16[2,256,512]{2,1,0:T(8,128)(2,1)S(1)}, bf16[2,256,512]{2,1,0:T(8,128)(2,1)S(1)}, u32[]{:S(2)}, u32[]{:S(2)}) %collective-permute-start.59) | collective-permute-done | bytes 524320 | tf_op jit(solution)/shard_map/ppermute | solution.py:657
  285.7 3.4 %collective-permute-done.60.refs_7_ = bf16[2,288,512]{2,1,0:T(8,128)(2,1)S(1)} collective-permute-done((bf16[2,288,512]{2,1,0:T(8,128)(2,1)S(1)}, bf16[2,288,512]{2,1,0:T(8,128)(2,1)S(1)}, u32[]{:S(2)}, u32[]{:S(2)}) %collective-permute-start.60) | collective-permute-done | bytes 589856 | tf_op jit(solution)/shard_map/ppermute | solution.py:657
  289.2 5.9 %shard_map.359 = (f32[2048,512]{1,0:T(8,128)}, f32[512,2048]{1,0:T(8,128)}, f32[512,512]{1,0:T(8,128)}, f32[512,1536]{1,0:T(8,128)}, f32[1,512]{1,0:T(1,128)}, /...) custom-call(s32[16]{0:T(128)S(1)} %shift-right-arithmetic_and_fusion, ...), custom_call_target="tpu_custom_call" | custom-call | tf_op jit(solution)/shard_map/pallas_call | solution.py:647
  (305 shorter events, 110.6 us)
Async XLA Ops:
  0.7 19.7 %collective-permute-start.4 = (bf16[512,2048]{1,0:T(8,128)(2,1)}, bf16[512,2048]{1,0:T(8,128)(2,1)}, u32[]{:S(2)}, u32[]{:S(2)}) collective-permute-start(bf16[512,2048]{1,0:T(8,128)(2,1)} %bitcast.62), channel_id=1, source_target_pairs={{0,16},{16,0},{1,17},{17,1},{2,18},{18,2},{3,19},{19,3},{4,20},{20... | collective-permute-start | bytes 6291464 | tf_op jit(solution)/shard_map/ppermute | solution.py:711
  1.2 19.1 %collective-permute-start.5 = (bf16[2048,512]{1,0:T(8,128)(2,1)}, bf16[2048,512]{1,0:T(8,128)(2,1)}, u32[]{:S(2)}, u32[]{:S(2)}) collective-permute-start(bf16[2048,512]{1,0:T(8,128)(2,1)} %bitcast.64), channel_id=1, source_target_pairs={{0,16},{16,0},{1,17},{17,1},{2,18},{18,2},{3,19},{19,3},{4,20},{20... | collective-permute-start | bytes 6291464 | tf_op jit(solution)/shard_map/ppermute | solution.py:711
  4.5 15.0 %collective-permute-start.1 = (f32[12,512]{1,0:T(8,128)S(1)}, f32[12,512]{1,0:T(8,128)}, u32[]{:S(2)}, u32[]{:S(2)}) collective-permute-start(f32[12,512]{1,0:T(8,128)S(1)} %concatenate.63), channel_id=1, source_target_pairs={{0,16},{16,0},{1,17},{17,1},{2,18},{18,2},{3,19},{19,3},{4,20},{20... | collective-permute-start | bytes 73736 | tf_op jit(solution)/shard_map/ppermute | solution.py:711
  4.6 15.7 %collective-permute-start.2 = (bf16[512,1536]{1,0:T(8,128)(2,1)}, bf16[512,1536]{1,0:T(8,128)(2,1)}, u32[]{:S(2)}, u32[]{:S(2)}) collective-permute-start(bf16[512,1536]{1,0:T(8,128)(2,1)} %bitcast.68), channel_id=1, source_target_pairs={{0,16},{16,0},{1,17},{17,1},{2,18},{18,2},{3,19},{19,3},{4,20},{20... | collective-permute-start | bytes 4718600 | tf_op jit(solution)/shard_map/ppermute | solution.py:711
  98.7 15.3 %collective-permute-start.8 = (bf16[2304,512]{1,0:T(8,128)(2,1)}, bf16[2304,512]{1,0:T(8,128)(2,1)}, u32[]{:S(2)}, u32[]{:S(2)}) collective-permute-start(bf16[2304,512]{1,0:T(8,128)(2,1)} %get-tuple-element.203), channel_id=1, source_target_pairs={{0,16},{16,0},{1,17},{17,1},{2,18},{18,2},{3,19},{19,3},{4,20},{20... | collective-permute-start | bytes 7077896 | tf_op jit(solution)/shard_map/ppermute | solution.py:711
  98.9 28.7 %collective-permute-start.26 = (bf16[2304,512]{1,0:T(8,128)(2,1)}, bf16[2304,512]{1,0:T(8,128)(2,1)}, u32[]{:S(2)}, u32[]{:S(2)}) collective-permute-start(bf16[2304,512]{1,0:T(8,128)(2,1)} %get-tuple-element.240), channel_id=1, source_target_pairs={{0,16},{16,0},{1,17},{17,1},{2,18},{18,2},{3,19},{19,3},{4,20},{20... | collective-permute-start | bytes 7077896 | tf_op jit(solution)/shard_map/ppermute | solution.py:711
  113.6 19.0 %collective-permute-start.27 = (bf16[768,512]{1,0:T(8,128)(2,1)}, bf16[768,512]{1,0:T(8,128)(2,1)}, u32[]{:S(2)}, u32[]{:S(2)}) collective-permute-start(bf16[768,512]{1,0:T(8,128)(2,1)} %get-tuple-element.245), channel_id=1, source_target_pairs={{0,16},{16,0},{1,17},{17,1},{2,18},{18,2},{3,19},{19,3},{4,20},{20... | collective-permute-start | bytes 2359304 | tf_op jit(solution)/shard_map/ppermute | solution.py:711
  118.9 31.3 %collective-permute-start.10 = (bf16[512,512]{1,0:T(8,128)(2,1)}, bf16[512,512]{1,0:T(8,128)(2,1)}, u32[]{:S(2)}, u32[]{:S(2)}) collective-permute-start(bf16[512,512]{1,0:T(8,128)(2,1)} %get-tuple-element.211), channel_id=1, source_target_pairs={{0,1},{1,0},{2,3},{3,2},{4,5},{5,4},{6,7},{7,6},{8,9},{9,8},{10,11... | collective-permute-start | bytes 1572872 | tf_op jit(solution)/shard_map/ppermute | solution.py:657
  121.8 28.9 %collective-permute-start.11 = (bf16[512,512]{1,0:T(8,128)(2,1)}, bf16[512,512]{1,0:T(8,128)(2,1)}, u32[]{:S(2)}, u32[]{:S(2)}) collective-permute-start(bf16[512,512]{1,0:T(8,128)(2,1)} %get-tuple-element.212), channel_id=1, source_target_pairs={{0,2},{1,3},{2,0},{3,1},{4,6},{5,7},{6,4},{7,5},{8,10},{9,11},{10,... | collective-permute-start | bytes 1572872 | tf_op jit(solution)/shard_map/ppermute | solution.py:657
  126.1 13.8 %collective-permute-start.12 = (bf16[256,512]{1,0:T(8,128)(2,1)S(1)}, bf16[256,512]{1,0:T(8,128)(2,1)S(1)}, u32[]{:S(2)}, u32[]{:S(2)}) collective-permute-start(bf16[256,512]{1,0:T(8,128)(2,1)S(1)} %get-tuple-element.213), channel_id=1, source_target_pairs={{0,4},{1,5},{2,6},{3,7},{4,0},{5,1},{6,2},{7,3},{8,12},{9,13},{10,... | collective-permute-start | bytes 786440 | tf_op jit(solution)/shard_map/ppermute | solution.py:657
  127.7 22.0 %collective-permute-start.13 = (bf16[256,512]{1,0:T(8,128)(2,1)}, bf16[256,512]{1,0:T(8,128)(2,1)}, u32[]{:S(2)}, u32[]{:S(2)}) collective-permute-start(bf16[256,512]{1,0:T(8,128)(2,1)} %get-tuple-element.214), channel_id=1, source_target_pairs={{0,8},{1,9},{2,10},{3,11},{4,12},{5,13},{6,14},{7,15},{8,0},{9,1},... | collective-permute-start | bytes 786440 | tf_op jit(solution)/shard_map/ppermute | solution.py:657
  136.6 24.2 %collective-permute-start.30 = (bf16[256,512]{1,0:T(8,128)(2,1)}, bf16[256,512]{1,0:T(8,128)(2,1)}, u32[]{:S(2)}, u32[]{:S(2)}) collective-permute-start(bf16[256,512]{1,0:T(8,128)(2,1)} %get-tuple-element.250), channel_id=1, source_target_pairs={{0,4},{1,5},{2,6},{3,7},{4,0},{5,1},{6,2},{7,3},{8,12},{9,13},{10,... | collective-permute-start | bytes 786440 | tf_op jit(solution)/shard_map/ppermute | solution.py:657
  140.5 21.1 %collective-permute-start.31 = (bf16[256,512]{1,0:T(8,128)(2,1)}, bf16[256,512]{1,0:T(8,128)(2,1)}, u32[]{:S(2)}, u32[]{:S(2)}) collective-permute-start(bf16[256,512]{1,0:T(8,128)(2,1)} %get-tuple-element.251), channel_id=1, source_target_pairs={{0,8},{1,9},{2,10},{3,11},{4,12},{5,13},{6,14},{7,15},{8,0},{9,1},... | collective-permute-start | bytes 786440 | tf_op jit(solution)/shard_map/ppermute | solution.py:657
  149.7 20.8 %collective-permute-start.28 = (bf16[512,512]{1,0:T(8,128)(2,1)}, bf16[512,512]{1,0:T(8,128)(2,1)}, u32[]{:S(2)}, u32[]{:S(2)}) collective-permute-start(bf16[512,512]{1,0:T(8,128)(2,1)} %copy-done.46), channel_id=1, source_target_pairs={{0,1},{1,0},{2,3},{3,2},{4,5},{5,4},{6,7},{7,6},{8,9},{9,8},{10,11... | collective-permute-start | bytes 1572872 | tf_op jit(solution)/shard_map/ppermute | solution.py:657
  150.2 21.8 %collective-permute-start.29 = (bf16[512,512]{1,0:T(8,128)(2,1)}, bf16[512,512]{1,0:T(8,128)(2,1)}, u32[]{:S(2)}, u32[]{:S(2)}) collective-permute-start(bf16[512,512]{1,0:T(8,128)(2,1)} %copy-done.45), channel_id=1, source_target_pairs={{0,2},{1,3},{2,0},{3,1},{4,6},{5,7},{6,4},{7,5},{8,10},{9,11},{10,... | collective-permute-start | bytes 1572872 | tf_op jit(solution)/shard_map/ppermute | solution.py:657
  159.3 20.5 %collective-permute-start.14 = (bf16[256,512]{1,0:T(8,128)(2,1)}, bf16[256,512]{1,0:T(8,128)(2,1)}, u32[]{:S(2)}, u32[]{:S(2)}) collective-permute-start(bf16[256,512]{1,0:T(8,128)(2,1)} %get-tuple-element.219), channel_id=1, source_target_pairs={{0,2},{1,3},{2,0},{3,1},{4,6},{5,7},{6,4},{7,5},{8,10},{9,11},{10,... | collective-permute-start | bytes 786440 | tf_op jit(solution)/shard_map/ppermute | solution.py:657
  160.8 15.6 %collective-permute-start.16 = (bf16[128,512]{1,0:T(8,128)(2,1)}, bf16[128,512]{1,0:T(8,128)(2,1)}, u32[]{:S(2)}, u32[]{:S(2)}) collective-permute-start(bf16[128,512]{1,0:T(8,128)(2,1)} %get-tuple-element.221), channel_id=1, source_target_pairs={{0,8},{1,9},{2,10},{3,11},{4,12},{5,13},{6,14},{7,15},{8,0},{9,1},... | collective-permute-start | bytes 393224 | tf_op jit(solution)/shard_map/ppermute | solution.py:657
  161.7 15.3 %collective-permute-start.17 = (bf16[128,512]{1,0:T(8,128)(2,1)}, bf16[128,512]{1,0:T(8,128)(2,1)}, u32[]{:S(2)}, u32[]{:S(2)}) collective-permute-start(bf16[128,512]{1,0:T(8,128)(2,1)} %get-tuple-element.222), channel_id=1, source_target_pairs={{0,4},{1,5},{2,6},{3,7},{4,0},{5,1},{6,2},{7,3},{8,12},{9,13},{10,... | collective-permute-start | bytes 393224 | tf_op jit(solution)/shard_map/ppermute | solution.py:657
  175.8 15.8 %collective-permute-start.32 = (bf16[256,512]{1,0:T(8,128)(2,1)S(1)}, bf16[256,512]{1,0:T(8,128)(2,1)S(1)}, u32[]{:S(2)}, u32[]{:S(2)}) collective-permute-start(bf16[256,512]{1,0:T(8,128)(2,1)S(1)} %get-tuple-element.256), channel_id=1, source_target_pairs={{0,2},{1,3},{2,0},{3,1},{4,6},{5,7},{6,4},{7,5},{8,10},{9,11},{10,... | collective-permute-start | bytes 786440 | tf_op jit(solution)/shard_map/ppermute | solution.py:657
  176.4 15.3 %collective-permute-start.33 = (bf16[256,512]{1,0:T(8,128)(2,1)S(1)}, bf16[256,512]{1,0:T(8,128)(2,1)S(1)}, u32[]{:S(2)}, u32[]{:S(2)}) collective-permute-start(bf16[256,512]{1,0:T(8,128)(2,1)S(1)} %get-tuple-element.257), channel_id=1, source_target_pairs={{0,1},{1,0},{2,3},{3,2},{4,5},{5,4},{6,7},{7,6},{8,9},{9,8},{10,11... | collective-permute-start | bytes 786440 | tf_op jit(solution)/shard_map/ppermute | solution.py:657
  181.2 14.7 %collective-permute-start.18 = (bf16[128,512]{1,0:T(8,128)(2,1)S(1)}, bf16[128,512]{1,0:T(8,128)(2,1)S(1)}, u32[]{:S(2)}, u32[]{:S(2)}) collective-permute-start(bf16[128,512]{1,0:T(8,128)(2,1)S(1)} %get-tuple-element.227), channel_id=1, source_target_pairs={{0,4},{1,5},{2,6},{3,7},{4,0},{5,1},{6,2},{7,3},{8,12},{9,13},{10,... | collective-permute-start | bytes 393224 | tf_op jit(solution)/shard_map/ppermute | solution.py:657
  225.7 12.4 %collective-permute-start.49 = (bf16[2,128,512]{2,1,0:T(8,128)(2,1)S(1)}, bf16[2,128,512]{2,1,0:T(8,128)(2,1)S(1)}, u32[]{:S(2)}, u32[]{:S(2)}) collective-permute-start(bf16[2,128,512]{2,1,0:T(8,128)(2,1)S(1)} %get-tuple-element.292.refs_0_), channel_id=1, source_target_pairs={{0,4},{1,5},{2,6},{3,7},{4,0},{5,1},{6,2},{7,3},{8,12},{9,13},{10,... | collective-permute-start | bytes 786440 | tf_op jit(solution)/shard_map/ppermute | solution.py:657
  225.8 14.7 %collective-permute-start.50 = (bf16[2,128,512]{2,1,0:T(8,128)(2,1)S(1)}, bf16[2,128,512]{2,1,0:T(8,128)(2,1)S(1)}, u32[]{:S(2)}, u32[]{:S(2)}) collective-permute-start(bf16[2,128,512]{2,1,0:T(8,128)(2,1)S(1)} %get-tuple-element.293.refs_1_), channel_id=1, source_target_pairs={{0,8},{1,9},{2,10},{3,11},{4,12},{5,13},{6,14},{7,15},{8,0},{9,1},... | collective-permute-start | bytes 786440 | tf_op jit(solution)/shard_map/ppermute | solution.py:657
  241.2 14.9 %collective-permute-start.53 = (bf16[2,256,512]{2,1,0:T(8,128)(2,1)S(1)}, bf16[2,256,512]{2,1,0:T(8,128)(2,1)S(1)}, u32[]{:S(2)}, u32[]{:S(2)}) collective-permute-start(bf16[2,256,512]{2,1,0:T(8,128)(2,1)S(1)} %get-tuple-element.296.refs_0_), channel_id=1, source_target_pairs={{0,2},{1,3},{2,0},{3,1},{4,6},{5,7},{6,4},{7,5},{8,10},{9,11},{10,... | collective-permute-start | bytes 1572872 | tf_op jit(solution)/shard_map/ppermute | solution.py:657
  241.7 14.4 %collective-permute-start.54 = (bf16[2,256,512]{2,1,0:T(8,128)(2,1)S(1)}, bf16[2,256,512]{2,1,0:T(8,128)(2,1)S(1)}, u32[]{:S(2)}, u32[]{:S(2)}) collective-permute-start(bf16[2,256,512]{2,1,0:T(8,128)(2,1)S(1)} %get-tuple-element.297.refs_1_), channel_id=1, source_target_pairs={{0,1},{1,0},{2,3},{3,2},{4,5},{5,4},{6,7},{7,6},{8,9},{9,8},{10,11... | collective-permute-start | bytes 1572872 | tf_op jit(solution)/shard_map/ppermute | solution.py:657
  242.3 13.8 %collective-permute-start.56 = (bf16[2,160,512]{2,1,0:T(8,128)(2,1)S(1)}, bf16[2,160,512]{2,1,0:T(8,128)(2,1)S(1)}, u32[]{:S(2)}, u32[]{:S(2)}) collective-permute-start(bf16[2,160,512]{2,1,0:T(8,128)(2,1)S(1)} %get-tuple-element.299.refs_3_), channel_id=1, source_target_pairs={{0,4},{1,5},{2,6},{3,7},{4,0},{5,1},{6,2},{7,3},{8,12},{9,13},{10,... | collective-permute-start | bytes 983048 | tf_op jit(solution)/shard_map/ppermute | solution.py:657
  242.3 11.6 %collective-permute-start.55 = (bf16[2,128,512]{2,1,0:T(8,128)(2,1)S(1)}, bf16[2,128,512]{2,1,0:T(8,128)(2,1)S(1)}, u32[]{:S(2)}, u32[]{:S(2)}) collective-permute-start(bf16[2,128,512]{2,1,0:T(8,128)(2,1)S(1)} %get-tuple-element.298.refs_2_), channel_id=1, source_target_pairs={{0,8},{1,9},{2,10},{3,11},{4,12},{5,13},{6,14},{7,15},{8,0},{9,1},... | collective-permute-start | bytes 786440 | tf_op jit(solution)/shard_map/ppermute | solution.py:657
  245.3 18.3 %collective-permute-start.7 = (f32[2,196,512]{2,0,1:T(2,128)S(1)}, f32[2,196,512]{2,0,1:T(2,128)S(1)}, u32[]{:S(2)}, u32[]{:S(2)}) collective-permute-start(f32[2,196,512]{2,0,1:T(2,128)S(1)} %copy.64), channel_id=1, source_target_pairs={{0,16},{16,0},{1,17},{17,1},{2,18},{18,2},{3,19},{19,3},{4,20},{20... | collective-permute-start | bytes 2408456 | tf_op jit(solution)/shard_map/ppermute | solution.py:711
  256.9 32.3 %collective-permute-start.57 = (bf16[2,512,512]{2,1,0:T(8,128)(2,1)S(1)}, bf16[2,512,512]{2,1,0:T(8,128)(2,1)S(1)}, u32[]{:S(2)}, u32[]{:S(2)}) collective-permute-start(bf16[2,512,512]{2,1,0:T(8,128)(2,1)S(1)} %get-tuple-element.300.refs_0_), channel_id=1, source_target_pairs={{0,1},{1,0},{2,3},{3,2},{4,5},{5,4},{6,7},{7,6},{8,9},{9,8},{10,11... | collective-permute-start | bytes 3145736 | tf_op jit(solution)/shard_map/ppermute | solution.py:657
  258.3 30.8 %collective-permute-start.58 = (bf16[2,512,512]{2,1,0:T(8,128)(2,1)S(1)}, bf16[2,512,512]{2,1,0:T(8,128)(2,1)S(1)}, u32[]{:S(2)}, u32[]{:S(2)}) collective-permute-start(bf16[2,512,512]{2,1,0:T(8,128)(2,1)S(1)} %get-tuple-element.301.refs_1_), channel_id=1, source_target_pairs={{0,2},{1,3},{2,0},{3,1},{4,6},{5,7},{6,4},{7,5},{8,10},{9,11},{10,... | collective-permute-start | bytes 3145736 | tf_op jit(solution)/shard_map/ppermute | solution.py:657
  260.0 29.2 %collective-permute-start.60 = (bf16[2,288,512]{2,1,0:T(8,128)(2,1)S(1)}, bf16[2,288,512]{2,1,0:T(8,128)(2,1)S(1)}, u32[]{:S(2)}, u32[]{:S(2)}) collective-permute-start(bf16[2,288,512]{2,1,0:T(8,128)(2,1)S(1)} %get-tuple-element.303.refs_3_), channel_id=1, source_target_pairs={{0,8},{1,9},{2,10},{3,11},{4,12},{5,13},{6,14},{7,15},{8,0},{9,1},... | collective-permute-start | bytes 1769480 | tf_op jit(solution)/shard_map/ppermute | solution.py:657
  261.8 24.0 %collective-permute-start.59 = (bf16[2,256,512]{2,1,0:T(8,128)(2,1)S(1)}, bf16[2,256,512]{2,1,0:T(8,128)(2,1)S(1)}, u32[]{:S(2)}, u32[]{:S(2)}) collective-permute-start(bf16[2,256,512]{2,1,0:T(8,128)(2,1)S(1)} %get-tuple-element.302.refs_2_), channel_id=1, source_target_pairs={{0,4},{1,5},{2,6},{3,7},{4,0},{5,1},{6,2},{7,3},{8,12},{9,13},{10,... | collective-permute-start | bytes 1572872 | tf_op jit(solution)/shard_map/ppermute | solution.py:657
  (101 other events, 851.0 us)
